TPU v7x, 512 devices: a whole 4x8x8 slice. The times are simulated.
512 devices in a mesh: row: 128 (over y, z, core), col: 4 (over x).
Axes of the slice: x: 4, y: 8, z: 8, core: 2. Of those that a mesh axis runs over, the one named last changes fastest.
Arguments:
- feat_in: bfloat16 [4096, 256, 256], P('row', 'col'), may hold values from -6 to 6
- conv_weight: bfloat16 [2304, 256], P('col'), may hold values from -0.125 to 0.125
- conv_bias: float32 [256], replicated, may hold values from -4 to 4
- proj_weight: bfloat16 [256, 768], replicated, may hold values from -0.375 to 0.375
- qkv_weight: bfloat16 [768, 2304], P('row'), may hold values from -2 to 2
- tissue: int32 [2048, 128], P('row', 'col'), may hold values from 0 to 1, as said below
- phase: int32 [2048, 128], P('row', 'col'), may hold values from 0 to 3, as said below
Outputs:
- attended: bfloat16 [2048, 128, 768], P('row', 'col')
Inputs may be any that keep to these rules, and one draw needn't show every extreme that they name: Within each column strip, phase is the token column plus an offset drawn for each token row, modulo 4. In each device's block of tokens, every phase holds at least one tissue token.
All inputs are finite; a program needn't handle non-finite values.
Results may differ from a plain program's by a relative error of at most 0.0065.
Values may be sent and summed in bfloat16 or wider, within the bound.
A program may use at most 64 MiB of HBM per device.

v0:
```python
import jax
import jax.numpy as jnp
from jax import lax
from jax.sharding import PartitionSpec as P

HD = 64
DILATION_STEP = 4


def partner(array, axis, apart):
    return lax.ppermute(array, axis, [(i, i ^ 1 << apart) for i in range(lax.axis_size(axis))])


def shifted(array, axis, by):
    length = lax.axis_size(axis)
    pairs = [(i, i + by) for i in range(length) if 0 <= i + by < length]
    return lax.ppermute(array, axis, pairs)


def layer_norm(values):
    centred = values - jnp.mean(values, axis=-1, keepdims=True)
    spread_rows = jnp.mean(centred * centred, axis=-1, keepdims=True)
    return centred * lax.rsqrt(spread_rows + 1e-05)


def fold_rows(operand, piece):
    return jnp.dot(operand, piece, preferred_element_type=jnp.float32)


def split_pair(buffer, bit, mine):
    slots = buffer.shape[0]
    view = buffer.reshape((slots >> bit + 1, 2, 1 << bit) + buffer.shape[1:])
    keep = jnp.where(mine == 0, view[:, 0], view[:, 1])
    send = jnp.where(mine == 0, view[:, 1], view[:, 0])
    return (keep, send)


def join_pair(keep, got, mine, shape):
    first = jnp.where(mine == 0, keep, got)
    second = jnp.where(mine == 0, got, keep)
    return jnp.stack([first, second], axis=1).reshape(shape)


def route_sender(payload, flags):
    mine_index = lax.axis_index("row")
    for bit in range(flag_bits(flags)):
        mine = mine_index >> bit & 1
        keep_a, send_a = split_pair(payload, bit, mine)
        keep_b, send_b = split_pair(flags, bit, mine)
        got_a, got_b = partner((send_a, send_b), "row", bit)
        payload = join_pair(keep_a, got_a, mine, payload.shape)
        flags = join_pair(keep_b, got_b, mine, flags.shape)
    return (payload, flags)


def route_back(payload):
    mine_index = lax.axis_index("row")
    for bit in range(flag_bits(payload)):
        mine = mine_index >> bit & 1
        keep_a, send_a = split_pair(payload, bit, mine)
        got_a = partner(send_a, "row", bit)
        payload = join_pair(keep_a, got_a, mine, payload.shape)
    return payload


def flag_bits(buffer):
    return buffer.shape[0].bit_length() - 1


def attend(queries, keys_all, values_all, key_live, query_live):
    row_count = queries.shape[0]
    model_width = queries.shape[1]
    head_count = model_width // HD
    query_heads = queries.reshape(row_count, head_count, HD).transpose(1, 0, 2)
    key_heads = keys_all.reshape(keys_all.shape[0], head_count, HD).transpose(1, 0, 2)
    value_heads = values_all.reshape(values_all.shape[0], head_count, HD).transpose(1, 0, 2)
    allowed = (key_live > 0.5)[None, :]

    def one_head(operands):
        query_head, key_head, value_head = operands
        scores = jnp.einsum(
            "qd,kd->qk", query_head, key_head, preferred_element_type=jnp.float32
        ) * HD ** (-0.5)
        scores = jnp.where(allowed, scores, -1e30)
        top_score = jnp.max(scores, axis=1, keepdims=True)
        weights = jnp.where(allowed, jnp.exp(scores - top_score), 0.0)
        denominator = jnp.sum(weights, axis=1, keepdims=True)
        return (
            jnp.dot(weights.astype(jnp.bfloat16), value_head, preferred_element_type=jnp.float32)
            / denominator
        )

    stacked = lax.map(one_head, (query_heads, key_heads, value_heads))
    merged = stacked.transpose(1, 0, 2).reshape(row_count, model_width)
    return (merged * query_live.astype(jnp.float32)[:, None]).astype(jnp.bfloat16)


def local(feat_in, conv_weight, conv_bias, proj_weight, qkv_weight, tissue, phase):
    in_rows, in_cols, channels = feat_in.shape
    out_rows = in_rows // 2
    out_cols = in_cols // 2
    token_count = out_rows * out_cols
    band_count = lax.axis_size("row")
    owner_labels = 2 * DILATION_STEP
    capacity = token_count // owner_labels
    model_width = qkv_weight.shape[0] * band_count
    left_edge = shifted(feat_in[:, in_cols - 1 :, :], "col", 1)
    widened = jnp.concatenate([left_edge, feat_in], axis=1)
    upper_edge = shifted(widened[in_rows - 1 :], "row", 1)
    padded = jnp.concatenate([upper_edge, widened], axis=0)
    windows = []
    for row_tap in range(3):
        for col_tap in range(3):
            window = padded[
                row_tap : row_tap + in_rows - 1 : 2, col_tap : col_tap + in_cols - 1 : 2, :
            ]
            windows.append(window.reshape(token_count, channels))
    patches = jnp.concatenate(windows, axis=1)
    conv_sum = fold_rows(patches, lax.all_gather(conv_weight, "col", axis=0, tiled=True))
    features = jax.nn.gelu(conv_sum + conv_bias).astype(jnp.bfloat16)
    tokens_bf = layer_norm(
        jnp.dot(features, proj_weight, preferred_element_type=jnp.float32)
    ).astype(jnp.bfloat16)
    phase_labels = phase.reshape(token_count)
    indicator_matrix = (
        phase_labels[:, None] == jnp.arange(DILATION_STEP, dtype=jnp.int32)[None, :]
    ).astype(jnp.int32)
    ranking = jnp.sum(
        (jnp.cumsum(indicator_matrix, axis=0) - indicator_matrix) * indicator_matrix, axis=1
    )
    target = (2 * phase_labels + ranking // capacity) * capacity + ranking % capacity
    inverse = (
        jnp.zeros((token_count,), jnp.int32)
        .at[target]
        .set(jnp.arange(token_count, dtype=jnp.int32))
    )
    tissue_flag = tissue.reshape(token_count).astype(jnp.bfloat16)
    flag_out = tissue_flag[inverse].reshape(owner_labels, capacity)
    qkv_local = fold_rows(tokens_bf, lax.all_gather(qkv_weight, "row", axis=0, tiled=True)).astype(
        jnp.bfloat16
    )
    arrived, arrived_flag = route_sender(
        qkv_local[inverse].reshape(owner_labels, capacity, 3 * model_width), flag_out
    )
    arrived_qkv = arrived.reshape(token_count, 3 * model_width)
    query_flag = arrived_flag.reshape(token_count)
    keys_values = arrived_qkv[:, model_width:]
    partner_kv, partner_flag = partner((keys_values, query_flag), "row", 0)
    joined_kv = jnp.concatenate([keys_values, partner_kv], axis=0)
    key_flag = jnp.concatenate([query_flag, partner_flag], axis=0)
    attended_rows = attend(
        arrived_qkv[:, :model_width],
        joined_kv[:, :model_width],
        joined_kv[:, model_width:],
        key_flag,
        query_flag,
    )
    returned = route_back(attended_rows.reshape(owner_labels, capacity, model_width))
    outputs = returned.reshape(token_count, model_width)[target]
    return outputs.reshape(out_rows, out_cols, model_width)


def solution(mesh):
    in_specs = (
        P("row", "col", None),
        P("col", None),
        P(),
        P(),
        P("row", None),
        P("row", "col"),
        P("row", "col"),
    )
    out_specs = P("row", "col", None)
    return jax.shard_map(local, mesh=mesh, in_specs=in_specs, out_specs=out_specs, check_vma=False)
```

profile of v0, /device:TPU:1, one launch (start us, length us, event | category | flops | bytes accessed | tf_op | source)
XLA Modules:
  0.0 378.8 jit_solution(9001759087257412841)
XLA Ops:
  9.0 3.9 %collective-permute-start.4 = (bf16[32,1,256]{2,1,0:T(2,128)(2,1)S(1)}, bf16[32,1,256]{2,1,0:T(2,128)(2,1)S(1)}, u32[]{:S(2)}, u32[]{:S(2)}) collective-permute-start(bf16[32,1,256]{2,1,0:T(2,128)(2,1)S(1)} %slice.131), channel_id=1, source_target_pairs={{0,1},{1,2},{2,3},{4,5},{5,6},{6,7},{8,9},{9,10},{10,11},{12,13},{... | collective-permute-start | bytes 49160 | tf_op jit(solution)/shard_map/ppermute | solution.py:17
  19.5 8.8 %slice.137 = bf16[16,32,256]{2,1,0:T(8,128)(2,1)} slice(bf16[32,64,256]{2,1,0:T(8,128)(2,1)} %param.9), slice={[0:31:2], [0:63:2], [0:256:1]} | slice | bytes 524288 | tf_op jit(solution)/shard_map/slice | solution.py:114
  28.2 7.0 %slice.138 = bf16[16,32,256]{2,1,0:T(8,128)(2,1)S(1)} slice(bf16[32,64,256]{2,1,0:T(8,128)(2,1)} %param.9), slice={[0:31:2], [1:64:2], [0:256:1]} | slice | bytes 524288 | tf_op jit(solution)/shard_map/slice | solution.py:114
  36.9 4.8 %collective-permute-start.5 = (bf16[1,65,256]{2,1,0:T(8,128)(2,1)S(1)}, bf16[1,65,256]{2,1,0:T(8,128)(2,1)S(1)}, u32[]{:S(2)}, u32[]{:S(2)}) collective-permute-start(bf16[1,65,256]{2,1,0:T(8,128)(2,1)S(1)} %fusion.51), channel_id=1, source_target_pairs={{0,4},{4,8},{8,12},{12,16},{16,20},{20,24},{24,28},{28,32},{32,36}... | collective-permute-start | bytes 99848 | tf_op jit(solution)/shard_map/ppermute | solution.py:17
  42.4 5.0 %slice.136 = bf16[16,32,256]{2,1,0:T(8,128)(2,1)} slice(bf16[32,65,256]{2,1,0:T(8,128)(2,1)S(1)} %pad_maximum_fusion.2), slice={[0:31:2], [0:63:2], [0:256:1]} | slice | bytes 524288 | tf_op jit(solution)/shard_map/slice | solution.py:114
  47.5 5.0 %slice.139 = bf16[16,32,256]{2,1,0:T(8,128)(2,1)} slice(bf16[32,65,256]{2,1,0:T(8,128)(2,1)S(1)} %pad_maximum_fusion.2), slice={[1:32:2], [0:63:2], [0:256:1]} | slice | bytes 524288 | tf_op jit(solution)/shard_map/slice | solution.py:114
  53.2 5.1 %slice.133 = bf16[16,32,256]{2,1,0:T(8,128)(2,1)} slice(bf16[33,65,256]{2,1,0:T(8,128)(2,1)S(1)} %maximum_maximum_fusion), slice={[0:31:2], [0:63:2], [0:256:1]} | slice | bytes 524288 | tf_op jit(solution)/shard_map/slice | solution.py:114
  58.3 5.0 %slice.134 = bf16[16,32,256]{2,1,0:T(8,128)(2,1)} slice(bf16[33,65,256]{2,1,0:T(8,128)(2,1)S(1)} %maximum_maximum_fusion), slice={[0:31:2], [1:64:2], [0:256:1]} | slice | bytes 524288 | tf_op jit(solution)/shard_map/slice | solution.py:114
  72.8 3.5 fusion.67
  76.6 57.6 %all-gather.6.cloned.1.call-done = bf16[128,6,2304]{2,1,0:T(8,128)(2,1)} async-done(((bf16[1,6,2304]{2,1,0:T(8,128)(2,1)}), bf16[128,6,2304]{2,1,0:T(8,128)(2,1)}) %all-gather.6.cloned.1.call-update) | async-done | bytes 3538960 | tf_op jit(solution)/shard_map/all_gather | solution.py:139
  134.2 6.6 %reshape.571 = bf16[768,2304]{1,0:T(8,128)(2,1)} reshape(bf16[128,6,2304]{2,1,0:T(8,128)(2,1)} %all-gather.6.cloned.1.call-done) | data formatting | bytes 7077888
  140.9 4.5 %convolution_convert_fusion = bf16[512,2304]{1,0:T(8,128)(2,1)S(1)} fusion(bf16[768,2304]{1,0:T(8,128)(2,1)} %reshape.571, f32[512,768]{1,0:T(8,128)} %copy-done.4, f32[512]{0:T(512)S(1)} %add_rsqrt_fusion, f32[512]{0:T(512)S(1)} %broadcast_multiply_fusion.1), kind=kOutput, calls=%fused_computation.28 | convolution fusion | flops 1814298624 | bytes 7475200 | tf_op jit(solution)/shard_map/dot_general | solution.py:27
  145.4 3.4 gather_fusion.1
  162.0 27.2 %collective-permute-done.7 = bf16[2,2,64,2304]{3,2,1,0:T(8,128)(2,1)} collective-permute-done((bf16[2,2,64,2304]{3,2,1,0:T(8,128)(2,1)}, bf16[2,2,64,2304]{3,2,1,0:T(8,128)(2,1)}, u32[]{:S(2)}, u32[]{:S(2)}) %collective-permute-start.7) | collective-permute-done | bytes 1179680 | tf_op jit(solution)/shard_map/ppermute | solution.py:11
  192.1 3.3 collective-permute-start.8
  195.5 3.5 gather_fusion
  199.1 49.2 %collective-permute-done.8 = bf16[1,4,64,2304]{3,2,1,0:T(8,128)(2,1)} collective-permute-done((bf16[1,4,64,2304]{3,2,1,0:T(8,128)(2,1)}, bf16[1,4,64,2304]{3,2,1,0:T(8,128)(2,1)}, u32[]{:S(2)}, u32[]{:S(2)}) %collective-permute-start.8) | collective-permute-done | bytes 1179680 | tf_op jit(solution)/shard_map/ppermute | solution.py:11
  266.6 4.7 %collective-permute-start.3 = (bf16[512]{0:T(512)(128)(2,1)S(1)}, bf16[512]{0:T(512)(128)(2,1)S(1)}, u32[]{:S(2)}, u32[]{:S(2)}) collective-permute-start(bf16[512]{0:T(512)(128)(2,1)S(1)} %reshape_reshape.30), channel_id=1, source_target_pairs={{0,4},{4,0},{8,12},{12,8},{16,20},{20,16},{24,28},{28,24},{32,36},... | collective-permute-start | bytes 3080 | tf_op jit(solution)/shard_map/ppermute | solution.py:11
  277.6 41.7 %while.10 = (s32[]{:T(128)}, f32[12,512,64]{1,2,0:T(8,128)}, pred[1,1024]{1,0:T(4,128)(4,1)S(1)}, bf16[12,512,64]{1,2,0:T(8,128)(2,1)}, bf16[12,1024,64]{1,2,0:T...) while((s32[]{:T(128)}, f32[12,512,64]{1,2,0:T(8,128)}, ...), condition=%wide.region_9.10_spmd, body=%wide.region_6.9_spmd.sunk | while | flops 141065216 | bytes 6767702 | solution.py:93
  319.2 3.6 reshape.533
  323.9 3.7 broadcast_select_fusion.1
  336.3 10.3 %collective-permute-done.11 = bf16[2,2,64,768]{3,2,1,0:T(8,128)(2,1)S(1)} collective-permute-done((bf16[2,2,64,768]{3,2,1,0:T(8,128)(2,1)S(1)}, bf16[2,2,64,768]{3,2,1,0:T(8,128)(2,1)S(1)}, u32[]{:S(2)}, u32[]{:S(2)}) %collective-permute-start.11) | collective-permute-done | bytes 393248 | tf_op jit(solution)/shard_map/ppermute | solution.py:11
  346.9 3.3 collective-permute-start.12
  350.3 18.8 %collective-permute-done.12 = bf16[1,4,64,768]{3,2,1,0:T(8,128)(2,1)S(1)} collective-permute-done((bf16[1,4,64,768]{3,2,1,0:T(8,128)(2,1)S(1)}, bf16[1,4,64,768]{3,2,1,0:T(8,128)(2,1)S(1)}, u32[]{:S(2)}, u32[]{:S(2)}) %collective-permute-start.12) | collective-permute-done | bytes 393248 | tf_op jit(solution)/shard_map/ppermute | solution.py:11
  (173 shorter events, 116.8 us)
Async XLA Ops:
  6.5 66.2 %copy-start = (bf16[256,768]{1,0:T(8,128)(2,1)S(1)}, bf16[256,768]{1,0:T(8,128)(2,1)}, u32[]{:S(2)}) copy-start(bf16[256,768]{1,0:T(8,128)(2,1)} %param.12) | copy-start | bytes 1179652
  6.5 28.7 %copy-start.3 = (bf16[32,64,256]{2,1,0:T(8,128)(2,1)S(1)}, bf16[32,64,256]{2,1,0:T(8,128)(2,1)}, u32[]{:S(2)}) copy-start(bf16[32,64,256]{2,1,0:T(8,128)(2,1)} %param.9) | copy-start | bytes 3145732
  6.5 66.2 %all-gather.4.cloned.1.call-start = ((), (), s32[]{:S(2)}) async-start(), calls=%async_computation | async-start | bytes 1474560 | tf_op jit(solution)/shard_map/all_gather | solution.py:119
  7.3 127.0 %all-gather.6.cloned.1.call-start = ((), (), s32[]{:S(2)}) async-start(), calls=%async_computation.1 | async-start | bytes 4755456 | tf_op jit(solution)/shard_map/all_gather | solution.py:139
  9.0 27.9 %collective-permute-start.4 = (bf16[32,1,256]{2,1,0:T(2,128)(2,1)S(1)}, bf16[32,1,256]{2,1,0:T(2,128)(2,1)S(1)}, u32[]{:S(2)}, u32[]{:S(2)}) collective-permute-start(bf16[32,1,256]{2,1,0:T(2,128)(2,1)S(1)} %slice.131), channel_id=1, source_target_pairs={{0,1},{1,2},{2,3},{4,5},{5,6},{6,7},{8,9},{9,10},{10,11},{12,13},{... | collective-permute-start | bytes 49160 | tf_op jit(solution)/shard_map/ppermute | solution.py:17
  36.9 15.6 %collective-permute-start.5 = (bf16[1,65,256]{2,1,0:T(8,128)(2,1)S(1)}, bf16[1,65,256]{2,1,0:T(8,128)(2,1)S(1)}, u32[]{:S(2)}, u32[]{:S(2)}) collective-permute-start(bf16[1,65,256]{2,1,0:T(8,128)(2,1)S(1)} %fusion.51), channel_id=1, source_target_pairs={{0,4},{4,8},{8,12},{12,16},{16,20},{20,24},{24,28},{28,32},{32,36}... | collective-permute-start | bytes 99848 | tf_op jit(solution)/shard_map/ppermute | solution.py:17
  53.2 15.0 %copy-start.7 = (bf16[16,32,256]{2,1,0:T(8,128)(2,1)S(1)}, bf16[16,32,256]{2,1,0:T(8,128)(2,1)}, u32[]{:S(2)}) copy-start(bf16[16,32,256]{2,1,0:T(8,128)(2,1)} %slice.136) | copy-start | bytes 786436
  58.3 10.7 %copy-start.5 = (bf16[16,32,256]{2,1,0:T(8,128)(2,1)S(1)}, bf16[16,32,256]{2,1,0:T(8,128)(2,1)}, u32[]{:S(2)}) copy-start(bf16[16,32,256]{2,1,0:T(8,128)(2,1)} %slice.137) | copy-start | bytes 786436
  63.9 6.6 %copy-start.6 = (bf16[16,32,256]{2,1,0:T(8,128)(2,1)S(1)}, bf16[16,32,256]{2,1,0:T(8,128)(2,1)}, u32[]{:S(2)}) copy-start(bf16[16,32,256]{2,1,0:T(8,128)(2,1)} %slice.139) | copy-start | bytes 786436
  68.2 4.6 %copy-start.9 = (f32[256]{0:T(256)S(1)}, f32[256]{0:T(256)}, u32[]{:S(2)}) copy-start(f32[256]{0:T(256)} %param.11) | copy-start | bytes 3076
  76.3 57.9 %copy-start.4 = (f32[512,768]{1,0:T(8,128)}, f32[512,768]{1,0:T(8,128)S(1)}, u32[]{:S(2)}) copy-start(f32[512,768]{1,0:T(8,128)S(1)} %get-tuple-element.113) | copy-start | bytes 4718596
  148.8 8.0 %copy-start.2 = (bf16[512,2304]{1,0:T(8,128)(2,1)S(1)}, bf16[512,2304]{1,0:T(8,128)(2,1)}, u32[]{:S(2)}) copy-start(bf16[512,2304]{1,0:T(8,128)(2,1)} %gather_fusion.1) | copy-start | bytes 7077892
  151.8 5.1 %collective-permute-start.6 = (bf16[4,1,64,2304]{3,2,0,1:T(8,128)(2,1)}, bf16[4,1,64,2304]{3,2,0,1:T(8,128)(2,1)}, u32[]{:S(2)}, u32[]{:S(2)}) collective-permute-start(bf16[4,1,64,2304]{3,2,0,1:T(8,128)(2,1)} %fusion.23), channel_id=1, source_target_pairs={{0,4},{4,0},{8,12},{12,8},{16,20},{20,16},{24,28},{28,24},{32,36},... | collective-permute-start | bytes 3538952 | tf_op jit(solution)/shard_map/ppermute | solution.py:11
  159.7 29.5 %collective-permute-start.7 = (bf16[2,2,64,2304]{3,2,1,0:T(8,128)(2,1)}, bf16[2,2,64,2304]{3,2,1,0:T(8,128)(2,1)}, u32[]{:S(2)}, u32[]{:S(2)}) collective-permute-start(bf16[2,2,64,2304]{3,2,1,0:T(8,128)(2,1)} %select_bitcast_fusion.1), channel_id=1, source_target_pairs={{0,8},{4,12},{8,0},{12,4},{16,24},{20,28},{24,16},{28,20},{32,40},... | collective-permute-start | bytes 3538952 | tf_op jit(solution)/shard_map/ppermute | solution.py:11
  190.9 4.5 %copy-start.8 = (s32[16,32]{1,0:T(8,128)S(1)}, s32[16,32]{1,0:T(8,128)}, u32[]{:S(2)}) copy-start(s32[16,32]{1,0:T(8,128)} %param.14) | copy-start | bytes 6148
  192.1 56.1 %collective-permute-start.8 = (bf16[1,4,64,2304]{3,2,1,0:T(8,128)(2,1)}, bf16[1,4,64,2304]{3,2,1,0:T(8,128)(2,1)}, u32[]{:S(2)}, u32[]{:S(2)}) collective-permute-start(bf16[1,4,64,2304]{3,2,1,0:T(8,128)(2,1)} %select_bitcast_fusion), channel_id=1, source_target_pairs={{0,16},{4,20},{8,24},{12,28},{16,0},{20,4},{24,8},{28,12},{32,48},... | collective-permute-start | bytes 3538952 | tf_op jit(solution)/shard_map/ppermute | solution.py:11
  251.3 21.8 %collective-permute-start.9 = (bf16[512,1536]{1,0:T(8,128)(2,1)}, bf16[512,1536]{1,0:T(8,128)(2,1)}, u32[]{:S(2)}, u32[]{:S(2)}) collective-permute-start(bf16[512,1536]{1,0:T(8,128)(2,1)} %slice.180), channel_id=1, source_target_pairs={{0,4},{4,0},{8,12},{12,8},{16,20},{20,16},{24,28},{28,24},{32,36},... | collective-permute-start | bytes 4718600 | tf_op jit(solution)/shard_map/ppermute | solution.py:11
  253.8 3.0 collective-permute-start
  256.9 4.3 %collective-permute-start.1 = (bf16[2,2,64]{2,1,0:T(2,128)(2,1)S(1)}, bf16[2,2,64]{2,1,0:T(2,128)(2,1)S(1)}, u32[]{:S(2)}, u32[]{:S(2)}) collective-permute-start(bf16[2,2,64]{2,1,0:T(2,128)(2,1)S(1)} %bitcast.242), channel_id=1, source_target_pairs={{0,8},{4,12},{8,0},{12,4},{16,24},{20,28},{24,16},{28,20},{32,40},... | collective-permute-start | bytes 1544 | tf_op jit(solution)/shard_map/ppermute | solution.py:11
  261.2 5.2 %collective-permute-start.2 = (bf16[1,4,64]{2,1,0:T(4,128)(2,1)S(1)}, bf16[1,4,64]{2,1,0:T(4,128)(2,1)S(1)}, u32[]{:S(2)}, u32[]{:S(2)}) collective-permute-start(bf16[1,4,64]{2,1,0:T(4,128)(2,1)S(1)} %select_bitcast_fusion.4), channel_id=1, source_target_pairs={{0,16},{4,20},{8,24},{12,28},{16,0},{20,4},{24,8},{28,12},{32,48},... | collective-permute-start | bytes 1544 | tf_op jit(solution)/shard_map/ppermute | solution.py:11
  266.6 5.3 %collective-permute-start.3 = (bf16[512]{0:T(512)(128)(2,1)S(1)}, bf16[512]{0:T(512)(128)(2,1)S(1)}, u32[]{:S(2)}, u32[]{:S(2)}) collective-permute-start(bf16[512]{0:T(512)(128)(2,1)S(1)} %reshape_reshape.30), channel_id=1, source_target_pairs={{0,4},{4,0},{8,12},{12,8},{16,20},{20,16},{24,28},{28,24},{32,36},... | collective-permute-start | bytes 3080 | tf_op jit(solution)/shard_map/ppermute | solution.py:11
  330.4 3.8 %collective-permute-start.10 = (bf16[4,1,64,768]{3,2,0,1:T(8,128)(2,1)}, bf16[4,1,64,768]{3,2,0,1:T(8,128)(2,1)S(1)}, u32[]{:S(2)}, u32[]{:S(2)}) collective-permute-start(bf16[4,1,64,768]{3,2,0,1:T(8,128)(2,1)} %bitcast.56), channel_id=1, source_target_pairs={{0,4},{4,0},{8,12},{12,8},{16,20},{20,16},{24,28},{28,24},{32,36},... | collective-permute-start | bytes 1179656 | tf_op jit(solution)/shard_map/ppermute | solution.py:11
  334.4 12.3 %collective-permute-start.11 = (bf16[2,2,64,768]{3,2,1,0:T(8,128)(2,1)S(1)}, bf16[2,2,64,768]{3,2,1,0:T(8,128)(2,1)S(1)}, u32[]{:S(2)}, u32[]{:S(2)}) collective-permute-start(bf16[2,2,64,768]{3,2,1,0:T(8,128)(2,1)S(1)} %select_bitcast_fusion.3), channel_id=1, source_target_pairs={{0,8},{4,12},{8,0},{12,4},{16,24},{20,28},{24,16},{28,20},{32,40},... | collective-permute-start | bytes 1179656 | tf_op jit(solution)/shard_map/ppermute | solution.py:11
  346.9 22.2 %collective-permute-start.12 = (bf16[1,4,64,768]{3,2,1,0:T(8,128)(2,1)S(1)}, bf16[1,4,64,768]{3,2,1,0:T(8,128)(2,1)S(1)}, u32[]{:S(2)}, u32[]{:S(2)}) collective-permute-start(bf16[1,4,64,768]{3,2,1,0:T(8,128)(2,1)S(1)} %select_bitcast_fusion.2), channel_id=1, source_target_pairs={{0,16},{4,20},{8,24},{12,28},{16,0},{20,4},{24,8},{28,12},{32,48},... | collective-permute-start | bytes 1179656 | tf_op jit(solution)/shard_map/ppermute | solution.py:11
  (1 other events, 2.7 us)
Sparse Core Ops, SparseCore 0:
  9.5 34.2 all-gather.3
  46.9 87.2 all-gather.5
where the time goes:
time: 381 us; the launch traced here: 379 us
  waiting for transfers between devices  174 us (46%)
  local copies, waits for them, and re-layouts  81.4 us (21%)
  matrix products  41.6 us (11%)
  starting transfers between devices  38 us (10%)
  other arithmetic  29.8 us (8%)
  between operations  13.9 us (4%)
    ppermute x11, waiting for transfers between devices, partner(): lax.ppermute(array, axis, [(i, i ^ 1 << apart) for i in range(lax.axis_si...  115 us
    all_gather x1, waiting for transfers between devices, local(): lax.all_gather(qkv_weight, 'row', axis=0, tiled=True)  57.6 us
    slice x9, local copies, waits for them, and re-layouts, local(): padded[row_tap:row_tap + in_rows - 1:2, col_tap:col_tap + in_cols - 1:2, :]  38.1 us
    ppermute x11, starting transfers between devices, partner(): lax.ppermute(array, axis, [(i, i ^ 1 << apart) for i in range(lax.axis_si...  29.2 us
    dot_general x12, matrix products, one_head(): jnp.einsum('qd,kd->qk', query_head, key_head, preferred_element_type=jnp....  17.8 us
    dot_general x12, matrix products, one_head(): jnp.dot(weights.astype(jnp.bfloat16), value_head, preferred_element_type=...  15.8 us
    unnamed x30, local copies, waits for them, and re-layouts  14.7 us
    ppermute x2, starting transfers between devices, shifted(): return lax.ppermute(array, axis, pairs)  8.79 us
  transfers between devices with their start and end apart: 15, of which 11 were waited for; matrix products, arithmetic and copies ran while one was open for 17% of the time, Pallas kernels for 0%

commit v1 on v0

v1 whole, which is shorter than its diff:
```python
import jax
import jax.numpy as jnp
from jax import lax
from jax.experimental import pallas as pl
from jax.experimental.pallas import tpu as pltpu
from jax.sharding import PartitionSpec as P

MESH = pl.DeviceIdType.MESH
F32 = jnp.float32
BF16 = jnp.bfloat16
ROWS = 128
COLS = 4
PLANE = 16
NY = 8
HALF = 1152
VMEM_LIMIT = 56 * 1024 * 1024


def iota(shape, dim):
    return lax.broadcasted_iota(jnp.int32, shape, dim)


def onehot(cond):
    return jnp.where(cond, 1.0, 0.0)


def dot(a, b):
    return jnp.dot(a, b, preferred_element_type=F32)


def dot_nt(a, b):
    return lax.dot_general(a, b, (((1,), (1,)), ((), ())), preferred_element_type=F32)


def dot_tn(a, b):
    return lax.dot_general(a, b, (((0,), (0,)), ((), ())), preferred_element_type=F32)


def remote(src, dst, send_sem, recv_sem, device):
    return pltpu.make_async_remote_copy(
        src_ref=src,
        dst_ref=dst,
        send_sem=send_sem,
        recv_sem=recv_sem,
        device_id=device,
        device_id_type=MESH,
    )


def greet(devices):
    barrier = pltpu.get_barrier_semaphore()
    for device in devices:
        pl.semaphore_signal(barrier, inc=1, device_id=device, device_id_type=MESH)
    pl.semaphore_wait(barrier, len(devices))


def conv_kernel(
    feat, cw, bias, w8, phase, tissue, fs, wc,
    grid_in, ext, halo, top, cwg, wsend, wz,
    cw_send, cw_recv, h_send, h_recv, z_send, z_recv, own_sem,
):
    row, col = lax.axis_index("row"), lax.axis_index("col")
    core = lax.rem(row, 2)
    base = row - lax.rem(row, PLANE)
    mine = row - base
    sibling = (base + lax.rem(mine, PLANE) + 1 - 2 * core, col)
    right, left = lax.rem(col + 1, COLS), lax.rem(col + COLS - 1, COLS)
    down, up = lax.rem(row + 1, ROWS), lax.rem(row + ROWS - 1, ROWS)
    plane = [(base + lax.rem(mine + k, PLANE), col) for k in range(1, PLANE)]
    greet(
        [(row, right), (row, left), (down, col), (up, col), (down, right), (up, left)]
        + plane
    )

    part = pl.multiple_of(core * 288, 32)

    def cw_piece(slot, start, size):
        return cwg.at[slot, pl.ds(pl.multiple_of(part + start, 16), size), :]

    across = lax.rem(col + 2, COLS)
    own = pltpu.make_async_copy(cw, cwg.at[col], own_sem)
    own.start()
    half = cw.at[pl.ds(part, 288), :]
    to_right = remote(half, cw_piece(col, 0, 288), cw_send.at[0], cw_recv.at[0], (row, right))
    to_left = remote(half, cw_piece(col, 0, 288), cw_send.at[1], cw_recv.at[1], (row, left))
    to_right.start()
    to_left.start()

    top_copy = remote(feat.at[31], top, h_send.at[0], h_recv.at[0], (down, col))
    top_copy.start()

    for c in range(2):
        for j in range(3):
            wsend[c, :, 384 * j : 384 * j + 384] = w8[
                :, 768 * j + 384 * c : 768 * j + 384 * c + 384
            ]
    z_copies = []
    for k in range(1, PLANE):
        to_core = lax.rem(core + k, 2)
        copy = remote(
            wsend.at[to_core], wz.at[mine], z_send.at[k], z_recv.at[k], plane[k - 1]
        )
        copy.start()
        z_copies.append(copy)
    own_z = pltpu.make_async_copy(wsend.at[core], wz.at[mine], z_recv.at[0])
    own_z.start()

    o, c = iota((256, 256), 0), iota((256, 256), 1)
    k, si, sp = o & 7, (o >> 3) & 3, (o >> 5) & 1
    r = 2 * ((o >> 6) & 1) + (o >> 7)
    split = onehot(c == r * 64 + 8 * k + 2 * si + sp).astype(BF16)
    for g in range(8):
        x = feat[4 * g : 4 * g + 4].reshape(256, 256)
        y = dot(split, x).reshape(2, 2, 2, 4, 8, 256)
        grid_in[0, 2 * g : 2 * g + 2, 0, 0:4] = y[0, :, 0]
        grid_in[0, 2 * g : 2 * g + 2, 1, 1:5] = y[0, :, 1]
        grid_in[1, 2 * g + 1 : 2 * g + 3, 0, 0:4] = y[1, :, 0]
        grid_in[1, 2 * g + 1 : 2 * g + 3, 1, 1:5] = y[1, :, 1]

    for rp in range(2):
        for i in range(0, 16, 8):
            rows8 = [grid_in[rp, rp + i + e, 1, 4, 7:8, :] for e in range(8)]
            ext[16 * rp + i : 16 * rp + i + 8, :] = jnp.concatenate(rows8, axis=0).astype(BF16)
    left_copy = remote(ext, halo.at[0:32], h_send.at[1], h_recv.at[1], (row, right))
    left_copy.start()
    corner_copy = remote(
        ext.at[24:32], halo.at[32:40], h_send.at[2], h_recv.at[2], (down, right)
    )
    corner_copy.start()

    to_right.wait_recv()
    on_right = remote(
        cw_piece(left, 0, 144), cw_piece(left, 0, 144), cw_send.at[2], cw_recv.at[2], (row, right)
    )
    on_right.start()
    sib_left = remote(
        cw_piece(left, 0, 288), cw_piece(left, 0, 288), cw_send.at[4], cw_recv.at[4], sibling
    )
    sib_left.start()
    to_left.wait_recv()
    on_left = remote(
        cw_piece(right, 144, 144), cw_piece(right, 144, 144), cw_send.at[3], cw_recv.at[3], (row, left)
    )
    on_left.start()
    sib_right = remote(
        cw_piece(right, 0, 288), cw_piece(right, 0, 288), cw_send.at[5], cw_recv.at[5], sibling
    )
    sib_right.start()

    top_copy.wait_recv()
    left_copy.wait_recv()
    corner_copy.wait_recv()
    below = row > 0
    inner = col > 0
    o, c = iota((64, 64), 0), iota((64, 64), 1)
    split_row = onehot(c == 8 * (o & 7) + 2 * ((o >> 3) & 3) + (o >> 5)).astype(BF16)
    yt = jnp.where(below, dot(split_row, top[...]), 0.0).reshape(2, 4, 8, 256)
    grid_in[1, 0, 0, 0:4] = yt[0]
    grid_in[1, 0, 1, 1:5] = yt[1]
    o, c = iota((272, 40), 0), iota((272, 40), 1)
    source = o >> 3
    source = jnp.where(source < 16, source, jnp.where(source == 16, 39, source - 1))
    spread = onehot((c == source) & ((o & 7) == 0)).astype(BF16)
    edge = jnp.where(inner, dot(spread, halo[...]), 0.0).reshape(34, 8, 256)
    first = iota((1, 8, 256), 1) == 0
    moved = pltpu.roll(grid_in[0, 0:16, 1, 4], 1, 1)
    grid_in[0, 0:16, 1, 0] = jnp.where(first, edge[0:16], moved)
    grid_in[0, 16, 1, 0] = jnp.zeros((8, 256), F32)
    moved = pltpu.roll(grid_in[1, 0:17, 1, 4], 1, 1)
    keep = edge[16:33]
    keep = jnp.where((iota((17, 8, 256), 0) == 0) & jnp.logical_not(below), 0.0, keep)
    grid_in[1, 0:17, 1, 0] = jnp.where(first, keep, moved)

    on_right.wait_recv()
    sib_on = remote(
        cw_piece(across, 0, 144), cw_piece(across, 0, 144), cw_send.at[6], cw_recv.at[6], sibling
    )
    sib_on.start()
    on_left.wait_recv()
    sib_off = remote(
        cw_piece(across, 144, 144), cw_piece(across, 144, 144), cw_send.at[7], cw_recv.at[7], sibling
    )
    sib_off.start()
    own.wait()
    for copy in (sib_left, sib_right, sib_on, sib_off):
        copy.wait_recv()

    weights = cwg[...].reshape(2304, 256)
    lane, sub = iota((8, 256), 1), iota((8, 256), 0)
    for h in range(2):
        pieces = []
        for a in range(3):
            for b in range(3):
                rp, i0 = (0, 0) if a == 1 else (1, a // 2)
                sp, m0 = (0, 0) if b == 1 else (1, b // 2)
                window = grid_in[rp, i0 + 8 * h : i0 + 8 * h + 8, sp, m0 : m0 + 4]
                pieces.append(window.reshape(256, 256).astype(BF16))
        pre = dot(jnp.concatenate(pieces, axis=1), weights) + bias[...]
        features = jax.nn.gelu(pre).astype(BF16)
        blocks = []
        for p in range(4):
            for i in range(8):
                target = i * 32 + ((p - phase[8 * h + i, 0]) & 3) * 8
                blocks.append(onehot(lane == sub + target))
        order = jnp.concatenate(blocks, axis=0).astype(BF16)
        fs[256 * h : 256 * h + 256, :] = dot(order, features).astype(BF16)
        j, c = iota((32, 256), 0), iota((32, 256), 1)
        pick = onehot(j == 4 * (c & 7) + ((c >> 3) & 3)).astype(BF16)
        flags = dot(tissue[8 * h : 8 * h + 8, :].astype(F32).astype(BF16), pick)
        flags = jnp.where(sub == (lane >> 5), flags, 0.0).astype(BF16)
        flags = dot(jnp.ones((8, 8), BF16), flags).astype(BF16)
        fs[512 + 8 * h : 520 + 8 * h, :] = dot_nt(flags, order).astype(BF16)

    own_z.wait()
    for copy in z_copies:
        copy.wait_recv()
    o, c = iota((96, 128), 0), iota((96, 128), 1)
    pack = onehot((o == 6 * (c >> 3) + (c & 7)) & ((c & 7) < 6)).astype(BF16)
    wc[...] = dot(pack, wz[...].reshape(128, HALF)).astype(BF16)

    for copy in z_copies + [
        to_right, to_left, on_right, on_left, sib_left, sib_right, sib_on, sib_off,
        top_copy, left_copy, corner_copy,
    ]:
        copy.wait_send()


def conv_call(feat, cw, bias, w8, phase, tissue):
    vmem = pl.BlockSpec(memory_space=pltpu.VMEM)
    return pl.pallas_call(
        conv_kernel,
        out_shape=(
            jax.ShapeDtypeStruct((528, 256), BF16),
            jax.ShapeDtypeStruct((96, HALF), BF16),
        ),
        in_specs=[vmem, vmem, vmem, vmem, pl.BlockSpec(memory_space=pltpu.SMEM), vmem],
        out_specs=(vmem, vmem),
        scratch_shapes=[
            pltpu.VMEM((2, 17, 2, 5, 8, 256), F32),
            pltpu.VMEM((32, 256), BF16),
            pltpu.VMEM((40, 256), BF16),
            pltpu.VMEM((64, 256), BF16),
            pltpu.VMEM((4, 576, 256), BF16),
            pltpu.VMEM((2, 8, HALF), BF16),
            pltpu.VMEM((16, 8, HALF), BF16),
            pltpu.SemaphoreType.DMA((8,)),
            pltpu.SemaphoreType.DMA((8,)),
            pltpu.SemaphoreType.DMA((3,)),
            pltpu.SemaphoreType.DMA((3,)),
            pltpu.SemaphoreType.DMA((16,)),
            pltpu.SemaphoreType.DMA((16,)),
            pltpu.SemaphoreType.DMA,
        ],
        compiler_params=pltpu.CompilerParams(
            collective_id=0, has_side_effects=True, vmem_limit_bytes=VMEM_LIMIT
        ),
        name="conv",
    )(feat, cw, bias, w8, phase, tissue)


def gather_kernel(
    fs, wc, slots, rings,
    r_send, r_recv, l_send, l_recv, s_send, s_recv, u_send, u_recv, d_send, d_recv, own,
):
    row, col = lax.axis_index("row"), lax.axis_index("col")
    core = lax.rem(row, 2)
    place = lax.rem(row // 2, 4)
    y = row // PLANE
    sibling = (row + 1 - 2 * core, col)
    ahead, behind = (lax.rem(row + 2, ROWS), col), (lax.rem(row + ROWS - 2, ROWS), col)
    above = (lax.rem(row + PLANE, ROWS), col)
    below = (lax.rem(row + ROWS - PLANE, ROWS), col)
    greet([sibling, ahead, behind, above, below])

    def ring(step):
        return lax.rem(y + step + NY, NY)

    own_f = pltpu.make_async_copy(fs, slots.at[0, 0], own.at[0])
    own_w = pltpu.make_async_copy(wc, rings.at[ring(0)], own.at[1])
    own_f.start()
    own_w.start()

    def f_right(t):
        src = fs if t == 0 else slots.at[4 - t, 0]
        return remote(src, slots.at[3 - t, 0], r_send.at[t], r_recv.at[t], ahead)

    def f_left(t):
        src = fs if t == 0 else slots.at[t, 0]
        return remote(src, slots.at[t + 1, 0], l_send.at[t], l_recv.at[t], behind)

    def f_sib(slot):
        src = fs if slot == 0 else slots.at[slot, 0]
        return remote(src, slots.at[slot, 1], s_send.at[slot], s_recv.at[slot], sibling)

    def w_up(t):
        slot = ring(-t)
        src = wc if t == 0 else rings.at[slot]
        dst = rings.at[slot]
        if t == 3:
            src, dst = rings.at[slot, 0:48], rings.at[slot, 0:48]
        return remote(src, dst, u_send.at[t], u_recv.at[t], above)

    def w_down(t):
        slot = ring(t)
        src = wc if t == 0 else rings.at[slot]
        dst = rings.at[slot]
        if t == 3:
            src, dst = rings.at[slot, 48:96], rings.at[slot, 48:96]
        return remote(src, dst, d_send.at[t], d_recv.at[t], below)

    @pl.when(place < 3)
    def _():
        f_right(0).start()

    @pl.when(place > 0)
    def _():
        f_left(0).start()

    w_up(0).start()
    w_down(0).start()
    f_sib(0).start()

    for t in range(1, 4):
        w_up(t - 1).wait_recv()
        w_up(t).start()
        w_down(t - 1).wait_recv()
        w_down(t).start()

        @pl.when(place >= t)
        def _():
            f_right(t - 1).wait_recv()
            f_sib(4 - t).start()

        if t < 3:

            @pl.when((place >= t) & (place < 3))
            def _():
                f_right(t).start()

        @pl.when(3 - place >= t)
        def _():
            f_left(t - 1).wait_recv()
            f_sib(t).start()

        if t < 3:

            @pl.when((3 - place >= t) & (place > 0))
            def _():
                f_left(t).start()

    w_up(3).wait_recv()
    w_down(3).wait_recv()
    own_f.wait()
    own_w.wait()
    for slot in range(4):
        f_sib(slot).wait_recv()
        f_sib(slot).wait_send()
    for t in range(4):
        w_up(t).wait_send()
        w_down(t).wait_send()
    for t in range(3):

        @pl.when((place >= t) & (place < 3))
        def _():
            f_right(t).wait_send()

        @pl.when((3 - place >= t) & (place > 0))
        def _():
            f_left(t).wait_send()


def gather_call(fs, wc):
    vmem = pl.BlockSpec(memory_space=pltpu.VMEM)
    return pl.pallas_call(
        gather_kernel,
        out_shape=(
            jax.ShapeDtypeStruct((4, 2, 528, 256), BF16),
            jax.ShapeDtypeStruct((NY, 96, HALF), BF16),
        ),
        in_specs=[vmem, vmem],
        out_specs=(vmem, vmem),
        scratch_shapes=[pltpu.SemaphoreType.DMA((4,))] * 10 + [pltpu.SemaphoreType.DMA((2,))],
        compiler_params=pltpu.CompilerParams(
            collective_id=1, has_side_effects=True, vmem_limit_bytes=VMEM_LIMIT
        ),
        name="gather",
    )(fs, wc)


def attend_kernel(slots, rings, proj, out, fold, gram, keys, values, dead, queries):
    w = rings[...].reshape(768, HALF)
    p32 = proj[...].astype(F32)
    mean_col = jnp.mean(p32, axis=1, keepdims=True)
    mean_row = dot_nt(jnp.ones((8, 768), BF16), proj[...])[0:1] * (1.0 / 768.0)
    col_sum = dot(jnp.ones((8, 768), BF16), w)[0:1]
    scale = jnp.where(iota((1, HALF), 1) < 384, 0.125 * 1.4426950408889634, 1.0)
    fold[...] = ((dot(proj[...], w) - mean_col * col_sum) * scale).astype(BF16)
    gram[...] = (dot_nt(proj[...], proj[...]) * (1.0 / 768.0) - mean_col * mean_row).astype(BF16)

    lane128 = iota((256, 128), 1)
    first_row = onehot((iota((8, 128), 0) == 0) & (iota((8, 128), 1) == 0)).astype(BF16)
    for q in range(4):
        for c in range(2):
            x = slots[q, c, 0:512, :]
            y = dot(x, gram[...])
            var = jnp.sum(y * x.astype(F32), axis=1, keepdims=True)
            rstd = lax.rsqrt(jnp.maximum(var, 0.0) + 1e-05)
            kv = (dot(x, fold[:, 384:]) * rstd).astype(BF16).reshape(2, 4, 64, 768)
            chunk = 4 * q + 2 * c
            for h in range(2):
                keys[:, chunk + h] = kv[h, :, :, 0:384]
                values[:, chunk + h] = kv[h, :, :, 384:768]
                live = dot_tn(slots[q, c, 512 + 8 * h : 520 + 8 * h, :], first_row)
                bias = jnp.where(lane128 == 0, (live - 1.0) * 1e30, 0.0)
                dead[:, chunk + h] = bias.astype(BF16).reshape(4, 64, 128)
            if q == 0:
                qs = (dot(x, fold[:, 0:384]) * rstd).astype(BF16).reshape(2, 4, 64, 384)
                for h in range(2):
                    queries[:, 2 * c + h] = qs[h]

    lane = iota((256, 128), 1)
    unit = onehot(lane == 0).astype(BF16)
    ones = jnp.ones((1024, 128), BF16)

    def one_phase(p, carry):
        k_all = keys[p].reshape(1024, 384)
        v_all = values[p].reshape(1024, 384)
        q_all = queries[p].reshape(256, 384)
        mask = dead[p].reshape(1024, 128)
        for n in range(3):
            cut = slice(128 * n, 128 * n + 128)
            k_pair = jnp.concatenate([k_all[:, cut], mask], axis=1)
            v_pair = jnp.concatenate([v_all[:, cut], ones], axis=1)
            q_pair = q_all[:, cut].astype(F32)
            both = []
            for e in range(2):
                q_head = jnp.where((lane >= 64) == (e == 1), q_pair, 0.0).astype(BF16)
                scores = dot_nt(jnp.concatenate([q_head, unit], axis=1), k_pair)
                top = jnp.max(scores, axis=1, keepdims=True)
                weights = jnp.exp2(scores - top).astype(BF16)
                mixed = dot(weights, v_pair)
                both.append(mixed[:, 0:128] / mixed[:, 128:256])
            pair = jnp.where(lane < 64, both[0], both[1]).astype(BF16)
            out[p, :, cut] = pair
        return carry

    lax.fori_loop(0, 4, one_phase, 0)


def attend_call(slots, rings, proj):
    vmem = pl.BlockSpec(memory_space=pltpu.VMEM)
    return pl.pallas_call(
        attend_kernel,
        out_shape=jax.ShapeDtypeStruct((4, 256, 384), BF16),
        in_specs=[vmem] * 3,
        out_specs=vmem,
        scratch_shapes=[
            pltpu.VMEM((256, HALF), BF16),
            pltpu.VMEM((256, 256), BF16),
            pltpu.VMEM((4, 16, 64, 384), BF16),
            pltpu.VMEM((4, 16, 64, 384), BF16),
            pltpu.VMEM((4, 16, 64, 128), BF16),
            pltpu.VMEM((4, 4, 64, 384), BF16),
        ],
        compiler_params=pltpu.CompilerParams(vmem_limit_bytes=VMEM_LIMIT),
        name="attend",
    )(slots, rings, proj)


def order_kernel(mixed, flags, phase, out, theirs, send_sem, recv_sem):
    row, col = lax.axis_index("row"), lax.axis_index("col")
    core = lax.rem(row, 2)
    sibling = (row + 1 - 2 * core, col)
    greet([sibling])
    copy = remote(mixed.at[:, 128:256], theirs, send_sem, recv_sem, sibling)
    copy.start()
    orders = []
    j, lane = iota((32, 256), 0), iota((32, 256), 1)
    for h in range(2):
        blocks = []
        for i in range(8):
            p = ((j & 3) + phase[8 * h + i, 0]) & 3
            blocks.append(onehot(lane == p * 64 + i * 8 + (j >> 2)))
        live = flags[8 * h : 8 * h + 1, :].astype(F32)
        orders.append((jnp.concatenate(blocks, axis=0) * live).astype(BF16))
    copy.wait_recv()
    for h in range(2):
        a = mixed[:, 64 * h : 64 * h + 64].reshape(256, 384)
        b = theirs[:, 64 * h : 64 * h + 64].reshape(256, 384)
        a, b = dot(orders[h], a), dot(orders[h], b)
        lower = jnp.where(core == 0, a, b).astype(BF16).reshape(8, 32, 384)
        upper = jnp.where(core == 0, b, a).astype(BF16).reshape(8, 32, 384)
        out[8 * h : 8 * h + 8, :, 0:384] = lower
        out[8 * h : 8 * h + 8, :, 384:768] = upper
    copy.wait_send()


def order_call(mixed, flags, phase):
    vmem = pl.BlockSpec(memory_space=pltpu.VMEM)
    return pl.pallas_call(
        order_kernel,
        out_shape=jax.ShapeDtypeStruct((16, 32, 768), BF16),
        in_specs=[vmem, vmem, pl.BlockSpec(memory_space=pltpu.SMEM)],
        out_specs=vmem,
        scratch_shapes=[
            pltpu.VMEM((4, 128, 384), BF16),
            pltpu.SemaphoreType.DMA,
            pltpu.SemaphoreType.DMA,
        ],
        compiler_params=pltpu.CompilerParams(
            collective_id=2, has_side_effects=True, vmem_limit_bytes=VMEM_LIMIT
        ),
        name="order",
    )(mixed, flags, phase)


def local(feat_in, conv_weight, conv_bias, proj_weight, qkv_weight, tissue, phase):
    w8 = jnp.pad(qkv_weight, ((0, 2), (0, 0)))
    fs, wc = conv_call(feat_in, conv_weight, conv_bias.reshape(1, 256), w8, phase, tissue)
    slots, rings = gather_call(fs, wc)
    mixed = attend_call(slots, rings, proj_weight)
    return order_call(mixed, fs[512:528], phase)


def solution(mesh):
    in_specs = (
        P("row", "col", None),
        P("col", None),
        P(),
        P(),
        P("row", None),
        P("row", "col"),
        P("row", "col"),
    )
    out_specs = P("row", "col", None)
    return jax.shard_map(local, mesh=mesh, in_specs=in_specs, out_specs=out_specs, check_vma=False)
```

time: 381 us -> 86.9 us (0.23)
  waiting for transfers between devices: 174 us -> 0 us
  Pallas kernels: 0 us -> 81.8 us
  local copies, waits for them, and re-layouts: 81.4 us -> 4.75 us
  matrix products: 41.6 us -> 0 us
  starting transfers between devices: 38 us -> 0 us
  other arithmetic: 29.8 us -> 0 us
  between operations: 13.9 us -> 0.03 us
    ppermute x13 -> x0, waiting for transfers between devices: 115 us -> none  [the longest x11 115 us: partner(): lax.ppermute(array, axis, [(i, i ^ 1 << apart) for i in range(lax.axis_si...]
    pallas_call x0 -> x4, Pallas kernels: none -> 81.8 us  [the longest x1 30.3 us: gather_call(): pl.pallas_call(gather_kernel, out_shape=(jax.ShapeDtypeStruct((4, 2, 528,...]
    all_gather x2 -> x0, waiting for transfers between devices: 57.6 us -> none  [the longest x1 57.6 us: local(): lax.all_gather(qkv_weight, 'row', axis=0, tiled=True)]
    slice x16 -> x1, local copies, waits for them, and re-layouts: 44.2 us -> 1.29 us  [local(): return order_call(mixed, fs[512:528], phase)]
    dot_general x26 -> x0, matrix products: 41.6 us -> none  [the longest x12 17.8 us: one_head(): jnp.einsum('qd,kd->qk', query_head, key_head, preferred_element_type=jnp....]
    ppermute x13 -> x0, starting transfers between devices: 38 us -> none  [the longest x11 29.2 us: partner(): lax.ppermute(array, axis, [(i, i ^ 1 << apart) for i in range(lax.axis_si...]
    unnamed x30 -> x1, local copies, waits for them, and re-layouts: 14.7 us -> 2.06 us
    select_n x14 -> x0, other arithmetic: 10.7 us -> none  [the longest x6 5.39 us: split_pair(): send = jnp.where(mine == 0, view[:, 1], view[:, 0])]
  transfers between devices with their start and end apart: 15 -> 0, of which waited for: 11 -> 0; matrix products, arithmetic and copies ran while one was open for 17% -> 0% of each run, Pallas kernels for 0% -> 0%
where the time goes in v1:
time: 86.9 us; the launch traced here: 86.6 us
  Pallas kernels  81.8 us (94%)
  local copies, waits for them, and re-layouts  4.75 us (5%)
    pallas_call x1, Pallas kernels, gather_call(): pl.pallas_call(gather_kernel, out_shape=(jax.ShapeDtypeStruct((4, 2, 528,...  30.3 us
    pallas_call x1, Pallas kernels, conv_call(): pl.pallas_call(conv_kernel, out_shape=(jax.ShapeDtypeStruct((528, 256), B...  30.2 us
    pallas_call x1, Pallas kernels, attend_call(): pl.pallas_call(attend_kernel, out_shape=jax.ShapeDtypeStruct((4, 256, 384...  16.4 us
    pallas_call x1, Pallas kernels, order_call(): pl.pallas_call(order_kernel, out_shape=jax.ShapeDtypeStruct((16, 32, 768)...  4.9 us
    unnamed x1, local copies, waits for them, and re-layouts  2.06 us

profile of v1, /device:TPU:1, one launch (start us, length us, event | category | flops | bytes accessed | tf_op | source)
XLA Modules:
  0.0 86.6 jit_solution(3203329477225264997)
XLA Ops:
  0.0 1.4 %pad.4.w8 = bf16[8,2304]{1,0:T(8,128)(2,1)} pad(bf16[6,2304]{1,0:T(8,128)(2,1)} %param.11, bf16[]{:T(256)} %constant.2.clone.1), padding=0_2x0_0 | pad | bytes 64514 | tf_op jit(solution)/shard_map/jit(_pad)/pad | solution.py:518
  1.4 30.2 %conv.1 = (bf16[528,256]{1,0:T(8,128)(2,1)}, bf16[96,1152]{1,0:T(8,128)(2,1)}) custom-call(bf16[32,64,256]{2,1,0:T(8,128)(2,1)} %feat.1, bf16[576,256]{1,0:T(8,128)(2,1)} %cw.1, f32[1,256]{1,0:T(1,128)} %bitcast.1, bf16[8,2304]{1,0:T(8,128)(2,1)} %pad.4.w8, s32[16,32]{1,0:T(8,128)} %phase.3, s32[16,32]{1,0:T(8,128)} %tissue.1), custom_call_target="tpu_custom_call" | custom-call | tf_op jit(solution)/shard_map/conv/pallas_call | solution.py:230
  31.6 1.3 %slice.3.flags = bf16[16,256]{1,0:T(8,128)(2,1)} slice(bf16[528,256]{1,0:T(8,128)(2,1)} %get-tuple-element.9.fs), slice={[512:528], [0:256]} | slice | bytes 16384 | tf_op jit(solution)/shard_map/slice | solution.py:522
  32.9 30.3 %gather.1 = (bf16[4,2,528,256]{3,2,1,0:T(8,128)(2,1)}, bf16[8,96,1152]{2,1,0:T(8,128)(2,1)}) custom-call(bf16[528,256]{1,0:T(8,128)(2,1)} %get-tuple-element.9.fs, bf16[96,1152]{1,0:T(8,128)(2,1)} %get-tuple-element.10.wc), custom_call_target="tpu_custom_call" | custom-call | tf_op jit(solution)/shard_map/gather/pallas_call | solution.py:374
  63.2 16.4 %attend.1.mixed = bf16[4,256,384]{2,1,0:T(8,128)(2,1)} custom-call(bf16[4,2,528,256]{3,2,1,0:T(8,128)(2,1)} %get-tuple-element.11.slots, bf16[8,96,1152]{2,1,0:T(8,128)(2,1)} %get-tuple-element.12.rings, bf16[256,768]{1,0:T(8,128)(2,1)} %proj.1), custom_call_target="tpu_custom_call" | custom-call | tf_op jit(solution)/shard_map/attend/pallas_call | solution.py:452
  79.6 4.9 %order.1 = bf16[16,32,768]{2,1,0:T(8,128)(2,1)} custom-call(bf16[4,256,384]{2,1,0:T(8,128)(2,1)} %attend.1.mixed, bf16[16,256]{1,0:T(8,128)(2,1)} %slice.3.flags, s32[16,32]{1,0:T(8,128)} %phase.3), custom_call_target="tpu_custom_call" | custom-call | tf_op jit(solution)/shard_map/order/pallas_call | solution.py:500
  84.5 2.1 %copy.9 = bf16[16,32,768]{2,1,0:T(8,128)(2,1)} copy(bf16[16,32,768]{2,1,0:T(8,128)(2,1)} %order.1) | data formatting | bytes 1572864

commit v2 on v0

v2 whole, which is shorter than its diff:
```python
import jax
import jax.numpy as jnp
from jax import lax
from jax.experimental import pallas as pl
from jax.experimental.pallas import tpu as pltpu
from jax.sharding import PartitionSpec as P

MESH = pl.DeviceIdType.MESH
F32 = jnp.float32
BF16 = jnp.bfloat16
ROWS = 128
COLS = 4
PLANE = 16
NY = 8
HALF = 1152
VMEM_LIMIT = 56 * 1024 * 1024


def iota(shape, dim):
    return lax.broadcasted_iota(jnp.int32, shape, dim)


def onehot(cond):
    return jnp.where(cond, 1.0, 0.0)


def dot(a, b):
    return jnp.dot(a, b, preferred_element_type=F32)


def dot_nt(a, b):
    return lax.dot_general(a, b, (((1,), (1,)), ((), ())), preferred_element_type=F32)


def dot_tn(a, b):
    return lax.dot_general(a, b, (((0,), (0,)), ((), ())), preferred_element_type=F32)


def remote(src, dst, send_sem, recv_sem, device):
    return pltpu.make_async_remote_copy(
        src_ref=src,
        dst_ref=dst,
        send_sem=send_sem,
        recv_sem=recv_sem,
        device_id=device,
        device_id_type=MESH,
    )


def greet(devices):
    barrier = pltpu.get_barrier_semaphore()
    for device in devices:
        pl.semaphore_signal(barrier, inc=1, device_id=device, device_id_type=MESH)
    pl.semaphore_wait(barrier, len(devices))


def whole_kernel(
    feat, cw, bias, w6, proj, phase, tissue, out,
    grid_in, ext, halo, top, cwg, wsend, wz, rings, slots, flags, orders,
    fold, gram, keys, values, dead, queries, mixed, theirs,
    cw_send, cw_recv, h_send, h_recv, z_send, z_recv, g_send, g_recv,
    f_send, f_recv, s_send, s_recv, u_send, u_recv, d_send, d_recv, m_send, m_recv, own_sem,
):
    row, col = lax.axis_index("row"), lax.axis_index("col")
    core = lax.rem(row, 2)
    base = row - lax.rem(row, PLANE)
    mine = row - base
    y_at = row // PLANE
    place = lax.rem(row // 2, 4)
    sibling = (row + 1 - 2 * core, col)
    right, left = lax.rem(col + 1, COLS), lax.rem(col + COLS - 1, COLS)
    across = lax.rem(col + 2, COLS)
    down, up = lax.rem(row + 1, ROWS), lax.rem(row + ROWS - 1, ROWS)
    above = (lax.rem(row + PLANE, ROWS), col)
    below = (lax.rem(row + ROWS - PLANE, ROWS), col)
    plane = [(base + lax.rem(mine + k, PLANE), col) for k in range(1, PLANE)]
    greet(
        [(row, right), (row, left), (down, col), (up, col), (down, right), (up, left)]
        + [above, below]
        + plane
    )

    part = pl.multiple_of(core * 288, 32)

    def cw_piece(slot, start, size):
        return cwg.at[slot, pl.ds(pl.multiple_of(part + start, 16), size), :]

    def cw_copy(i, slot, start, size, device):
        piece = cw_piece(slot, start, size)
        return remote(piece, piece, cw_send.at[i], cw_recv.at[i], device)

    own_cw = pltpu.make_async_copy(cw, cwg.at[col], own_sem.at[0])
    own_cw.start()
    half = cw.at[pl.ds(part, 288), :]
    to_right = remote(half, cw_piece(col, 0, 288), cw_send.at[0], cw_recv.at[0], (row, right))
    to_left = remote(half, cw_piece(col, 0, 288), cw_send.at[1], cw_recv.at[1], (row, left))
    to_right.start()
    to_left.start()
    top_copy = remote(feat.at[31], top, h_send.at[0], h_recv.at[0], (down, col))
    top_copy.start()

    for c in range(2):
        wsend[c] = jnp.zeros((8, HALF), BF16)
        for j in range(3):
            wsend[c, 0:6, 384 * j : 384 * j + 384] = w6[
                :, 768 * j + 384 * c : 768 * j + 384 * c + 384
            ]
    z_copies = []
    for k in range(1, PLANE):
        to_core = lax.rem(core + k, 2)
        copy = remote(
            wsend.at[to_core], wz.at[mine], z_send.at[k], z_recv.at[k], plane[k - 1]
        )
        copy.start()
        z_copies.append(copy)
    own_z = pltpu.make_async_copy(wsend.at[core], wz.at[mine], own_sem.at[1])
    own_z.start()

    o, c = iota((256, 256), 0), iota((256, 256), 1)
    k, si, sp = o & 7, (o >> 3) & 3, (o >> 5) & 1
    r = 2 * ((o >> 6) & 1) + (o >> 7)
    split = onehot(c == r * 64 + 8 * k + 2 * si + sp).astype(BF16)
    for g in range(8):
        x = feat[4 * g : 4 * g + 4].reshape(256, 256)
        y = dot(split, x).reshape(2, 2, 2, 4, 8, 256)
        grid_in[0, 2 * g : 2 * g + 2, 0, 0:4] = y[0, :, 0]
        grid_in[0, 2 * g : 2 * g + 2, 1, 1:5] = y[0, :, 1]
        grid_in[1, 2 * g + 1 : 2 * g + 3, 0, 0:4] = y[1, :, 0]
        grid_in[1, 2 * g + 1 : 2 * g + 3, 1, 1:5] = y[1, :, 1]

    for rp in range(2):
        for i in range(0, 16, 8):
            rows8 = [grid_in[rp, rp + i + e, 1, 4, 7:8, :] for e in range(8)]
            ext[16 * rp + i : 16 * rp + i + 8, :] = jnp.concatenate(rows8, axis=0).astype(BF16)
    left_copy = remote(ext, halo.at[0:32], h_send.at[1], h_recv.at[1], (row, right))
    left_copy.start()
    corner_copy = remote(
        ext.at[24:32], halo.at[32:40], h_send.at[2], h_recv.at[2], (down, right)
    )
    corner_copy.start()

    lane, sub = iota((8, 256), 1), iota((8, 256), 0)
    for h in range(2):
        blocks = []
        for p in range(4):
            for i in range(8):
                target = i * 32 + ((p - phase[8 * h + i, 0]) & 3) * 8
                blocks.append(onehot(lane == sub + target))
        order = jnp.concatenate(blocks, axis=0).astype(BF16)
        orders[h] = order
        j, c = iota((32, 256), 0), iota((32, 256), 1)
        pick = onehot(j == 4 * (c & 7) + ((c >> 3) & 3)).astype(BF16)
        live = dot(tissue[8 * h : 8 * h + 8, :].astype(F32).astype(BF16), pick)
        live = jnp.where(sub == (lane >> 5), live, 0.0).astype(BF16)
        live = dot(jnp.ones((8, 8), BF16), live).astype(BF16)
        flags[0, 0, :, 256 * h : 256 * h + 256] = dot_nt(live, order).astype(BF16)
    g_copies = []
    for dz in range(4):
        for dc in range(2):
            if dz or dc:
                n = 2 * dz + dc
                peer = row + 2 * (lax.rem(place + dz, 4) - place) + dc * (1 - 2 * core)
                copy = remote(
                    flags.at[0, 0], flags.at[(4 - dz) % 4, dc], g_send.at[n], g_recv.at[n], (peer, col)
                )
                copy.start()
                g_copies.append(copy)

    to_right.wait_recv()
    on_right = cw_copy(2, left, 0, 144, (row, right))
    on_right.start()
    sib_left = cw_copy(4, left, 0, 288, sibling)
    sib_left.start()
    to_left.wait_recv()
    on_left = cw_copy(3, right, 144, 144, (row, left))
    on_left.start()
    sib_right = cw_copy(5, right, 0, 288, sibling)
    sib_right.start()

    own_z.wait()
    for copy in z_copies:
        copy.wait_recv()
    o, c = iota((96, 128), 0), iota((96, 128), 1)
    pack = onehot((o == 6 * (c >> 3) + (c & 7)) & ((c & 7) < 6)).astype(BF16)
    rings[y_at] = dot(pack, wz[...].reshape(128, HALF)).astype(BF16)

    def w_up(t):
        piece = rings.at[lax.rem(y_at + NY - t, NY)]
        piece = piece.at[0:48] if t == 3 else piece
        return remote(piece, piece, u_send.at[t], u_recv.at[t], above)

    def w_down(t):
        piece = rings.at[lax.rem(y_at + t, NY)]
        piece = piece.at[48:96] if t == 3 else piece
        return remote(piece, piece, d_send.at[t], d_recv.at[t], below)

    w_up(0).start()
    w_down(0).start()

    top_copy.wait_recv()
    left_copy.wait_recv()
    corner_copy.wait_recv()
    inside = row > 0
    inner = col > 0
    o, c = iota((64, 64), 0), iota((64, 64), 1)
    split_row = onehot(c == 8 * (o & 7) + 2 * ((o >> 3) & 3) + (o >> 5)).astype(BF16)
    yt = jnp.where(inside, dot(split_row, top[...]), 0.0).reshape(2, 4, 8, 256)
    grid_in[1, 0, 0, 0:4] = yt[0]
    grid_in[1, 0, 1, 1:5] = yt[1]
    o, c = iota((264, 40), 0), iota((264, 40), 1)
    source = o >> 3
    source = jnp.where(source < 16, source, jnp.where(source == 16, 39, source - 1))
    spread = onehot((c == source) & ((o & 7) == 0)).astype(BF16)
    edge = jnp.where(inner, dot(spread, halo[...]), 0.0).reshape(33, 8, 256)
    first = iota((1, 8, 256), 1) == 0
    moved = pltpu.roll(grid_in[0, 0:16, 1, 4], 1, 1)
    grid_in[0, 0:16, 1, 0] = jnp.where(first, edge[0:16], moved)
    moved = pltpu.roll(grid_in[1, 0:17, 1, 4], 1, 1)
    keep = edge[16:33]
    keep = jnp.where((iota((17, 8, 256), 0) == 0) & jnp.logical_not(inside), 0.0, keep)
    grid_in[1, 0:17, 1, 0] = jnp.where(first, keep, moved)

    on_right.wait_recv()
    sib_on = cw_copy(6, across, 0, 144, sibling)
    sib_on.start()
    on_left.wait_recv()
    sib_off = cw_copy(7, across, 144, 144, sibling)
    sib_off.start()
    own_cw.wait()
    for copy in (sib_left, sib_right, sib_on, sib_off):
        copy.wait_recv()

    weights = cwg[...].reshape(2304, 256)
    for h in range(2):
        pieces = []
        for a in range(3):
            for b in range(3):
                rp, i0 = (0, 0) if a == 1 else (1, a // 2)
                sp, m0 = (0, 0) if b == 1 else (1, b // 2)
                window = grid_in[rp, i0 + 8 * h : i0 + 8 * h + 8, sp, m0 : m0 + 4]
                pieces.append(window.reshape(256, 256).astype(BF16))
        pre = dot(jnp.concatenate(pieces, axis=1), weights) + bias[...]
        features = jax.nn.gelu(pre).astype(BF16)
        placed = dot(orders[h], features).astype(BF16).reshape(4, 64, 256)
        slots[0, 0, :, 64 * h : 64 * h + 64, :] = placed

    def f_right(p):
        return remote(
            slots.at[0, 0, p], slots.at[3, 0, p], f_send.at[0, p], f_recv.at[3, p],
            (lax.rem(row + 2, ROWS), col),
        )

    def f_left(p):
        return remote(
            slots.at[0, 0, p], slots.at[1, 0, p], f_send.at[1, p], f_recv.at[1, p],
            (lax.rem(row + ROWS - 2, ROWS), col),
        )

    def f_two(p):
        return remote(
            slots.at[0, 0, p], slots.at[2, 0, p], f_send.at[2, p], f_recv.at[2, p],
            (row + 4 * jnp.where(place < 2, 1, -1), col),
        )

    def f_far(p):
        to = jnp.where(place == 2, 1, 3)
        return remote(
            slots.at[2, 0, p], slots.at[to, 0, p], f_send.at[3, p], f_recv.at[to, p],
            (row + 2 * jnp.where(place == 2, 1, -1), col),
        )

    def f_sib(slot, p):
        piece = slots.at[slot, 0, p]
        return remote(piece, slots.at[slot, 1, p], s_send.at[slot, p], s_recv.at[slot, p], sibling)

    def arrived(slot, p):
        piece = slots.at[slot, 0, p]
        return remote(piece, piece, f_send.at[0, p], f_recv.at[slot, p], sibling)

    for p in range(4):

        @pl.when(place < 3)
        def _():
            f_right(p).start()

        @pl.when(place > 0)
        def _():
            f_left(p).start()

        f_two(p).start()
        f_sib(0, p).start()

    def serve(p):
        arrived(2, p).wait_recv()

        @pl.when((place == 1) | (place == 2))
        def _():
            f_far(p).start()

        f_sib(2, p).start()
        for slot in (1, 3):
            arrived(slot, p).wait_recv()
            f_sib(slot, p).start()

    p32 = proj[...].astype(F32)
    mean_col = jnp.mean(p32, axis=1, keepdims=True)
    mean_row = dot_nt(jnp.ones((8, 768), BF16), proj[...])[0:1] * (1.0 / 768.0)
    gram[...] = (dot_nt(proj[...], proj[...]) * (1.0 / 768.0) - mean_col * mean_row).astype(BF16)
    for copy in g_copies:
        copy.wait_recv()
    lane128 = iota((512, 128), 1)
    first_row = onehot((iota((8, 128), 0) == 0) & (iota((8, 128), 1) == 0)).astype(BF16)
    for q in range(4):
        for c in range(2):
            live = dot_tn(flags[q, c], first_row)
            gone = jnp.where((lane128 == 0) , (live - 1.0) * 1e30, 0.0).astype(BF16)
            gone = gone.reshape(2, 4, 64, 128)
            for h in range(2):
                dead[:, q, c, 64 * h : 64 * h + 64, :] = gone[h]

    w_up(0).wait_recv()
    w_up(1).start()
    w_down(0).wait_recv()
    w_down(1).start()
    serve(0)
    w_up(1).wait_recv()
    w_up(2).start()
    w_down(1).wait_recv()
    w_down(2).start()
    serve(1)
    w_up(2).wait_recv()
    w_up(3).start()
    w_down(2).wait_recv()
    w_down(3).start()
    w_up(3).wait_recv()
    w_down(3).wait_recv()

    w = rings[...].reshape(768, HALF)
    col_sum = dot(jnp.ones((8, 768), BF16), w)[0:1]
    scale = jnp.where(iota((1, HALF), 1) < 384, 0.125 * 1.4426950408889634, 1.0)
    fold[...] = ((dot(proj[...], w) - mean_col * col_sum) * scale).astype(BF16)

    lane = iota((256, 128), 1)
    unit = onehot(lane == 0).astype(BF16)
    ones = jnp.ones((1024, 128), BF16)

    def give(p):
        return remote(mixed.at[p, 128:256], theirs.at[p], m_send.at[p], m_recv.at[p], sibling)

    def one_phase(p, carry):
        for slot in range(4):
            f_sib(slot, p).wait_recv()
        x = slots[:, :, p].reshape(1024, 256)
        y = dot(x, gram[...])
        var = jnp.sum(y * x.astype(F32), axis=1, keepdims=True)
        rstd = lax.rsqrt(jnp.maximum(var, 0.0) + 1e-05)
        kv = (dot(x, fold[:, 384:]) * rstd).astype(BF16)
        keys[...] = kv[:, 0:384]
        values[...] = kv[:, 384:768]
        queries[...] = (dot(x[0:256], fold[:, 0:384]) * rstd[0:256]).astype(BF16)
        mask = dead[p].reshape(1024, 128)
        for n in range(3):
            if n == 1:

                @pl.when(p < 2)
                def _():
                    serve(p + 2)

            cut = slice(128 * n, 128 * n + 128)
            k_pair = jnp.concatenate([keys[:, cut], mask], axis=1)
            v_pair = jnp.concatenate([values[:, cut], ones], axis=1)
            q_pair = queries[:, cut].astype(F32)
            both = []
            for e in range(2):
                q_head = jnp.where((lane >= 64) == (e == 1), q_pair, 0.0).astype(BF16)
                scores = dot_nt(jnp.concatenate([q_head, unit], axis=1), k_pair)
                highest = jnp.max(scores, axis=1, keepdims=True)
                weights = jnp.exp2(scores - highest).astype(BF16)
                result = dot(weights, v_pair)
                both.append(result[:, 0:128] / result[:, 128:256])
            mixed[p, :, cut] = jnp.where(lane < 64, both[0], both[1]).astype(BF16)
        give(p).start()
        return carry

    lax.fori_loop(0, 4, one_phase, 0)

    back = []
    j, lane = iota((32, 256), 0), iota((32, 256), 1)
    for h in range(2):
        blocks = []
        for i in range(8):
            p = ((j & 3) + phase[8 * h + i, 0]) & 3
            blocks.append(onehot(lane == p * 64 + i * 8 + (j >> 2)))
        live = flags[0, 0, 0:1, 256 * h : 256 * h + 256].astype(F32)
        back.append((jnp.concatenate(blocks, axis=0) * live).astype(BF16))
    for p in range(4):
        give(p).wait_recv()
    for h in range(2):
        a = mixed[:, 64 * h : 64 * h + 64].reshape(256, 384)
        b = theirs[:, 64 * h : 64 * h + 64].reshape(256, 384)
        a, b = dot(back[h], a), dot(back[h], b)
        lower = jnp.where(core == 0, a, b).astype(BF16).reshape(8, 32, 384)
        upper = jnp.where(core == 0, b, a).astype(BF16).reshape(8, 32, 384)
        out[8 * h : 8 * h + 8, :, 0:384] = lower
        out[8 * h : 8 * h + 8, :, 384:768] = upper

    for copy in z_copies + g_copies + [
        to_right, to_left, on_right, on_left, sib_left, sib_right, sib_on, sib_off,
        top_copy, left_copy, corner_copy,
    ]:
        copy.wait_send()
    for t in range(4):
        w_up(t).wait_send()
        w_down(t).wait_send()
    for p in range(4):
        give(p).wait_send()
        f_two(p).wait_send()
        for slot in range(4):
            f_sib(slot, p).wait_send()

        @pl.when(place < 3)
        def _():
            f_right(p).wait_send()

        @pl.when(place > 0)
        def _():
            f_left(p).wait_send()

        @pl.when((place == 1) | (place == 2))
        def _():
            f_far(p).wait_send()


def local(feat_in, conv_weight, conv_bias, proj_weight, qkv_weight, tissue, phase):
    vmem = pl.BlockSpec(memory_space=pltpu.VMEM)
    dma = pltpu.SemaphoreType.DMA
    return pl.pallas_call(
        whole_kernel,
        out_shape=jax.ShapeDtypeStruct((16, 32, 768), BF16),
        in_specs=[vmem] * 5 + [pl.BlockSpec(memory_space=pltpu.SMEM), vmem],
        out_specs=vmem,
        scratch_shapes=[
            pltpu.VMEM((2, 17, 2, 5, 8, 256), F32),
            pltpu.VMEM((32, 256), BF16),
            pltpu.VMEM((40, 256), BF16),
            pltpu.VMEM((64, 256), BF16),
            pltpu.VMEM((4, 576, 256), BF16),
            pltpu.VMEM((2, 8, HALF), BF16),
            pltpu.VMEM((16, 8, HALF), BF16),
            pltpu.VMEM((NY, 96, HALF), BF16),
            pltpu.VMEM((4, 2, 4, 128, 256), BF16),
            pltpu.VMEM((4, 2, 8, 512), BF16),
            pltpu.VMEM((2, 256, 256), BF16),
            pltpu.VMEM((256, HALF), BF16),
            pltpu.VMEM((256, 256), BF16),
            pltpu.VMEM((1024, 384), BF16),
            pltpu.VMEM((1024, 384), BF16),
            pltpu.VMEM((4, 4, 2, 128, 128), BF16),
            pltpu.VMEM((256, 384), BF16),
            pltpu.VMEM((4, 256, 384), BF16),
            pltpu.VMEM((4, 128, 384), BF16),
            dma((8,)), dma((8,)),
            dma((3,)), dma((3,)),
            dma((16,)), dma((16,)),
            dma((8,)), dma((8,)),
            dma((4, 4)), dma((4, 4)),
            dma((4, 4)), dma((4, 4)),
            dma((4,)), dma((4,)),
            dma((4,)), dma((4,)),
            dma((4,)), dma((4,)),
            dma((2,)),
        ],
        compiler_params=pltpu.CompilerParams(
            collective_id=0, has_side_effects=True, vmem_limit_bytes=VMEM_LIMIT
        ),
        name="whole",
    )(
        feat_in, conv_weight, conv_bias.reshape(1, 256), qkv_weight, proj_weight, phase, tissue
    )


def solution(mesh):
    in_specs = (
        P("row", "col", None),
        P("col", None),
        P(),
        P(),
        P("row", None),
        P("row", "col"),
        P("row", "col"),
    )
    out_specs = P("row", "col", None)
    return jax.shard_map(local, mesh=mesh, in_specs=in_specs, out_specs=out_specs, check_vma=False)
```

time: 381 us -> 74.5 us (0.20)
  waiting for transfers between devices: 174 us -> 0 us
  local copies, waits for them, and re-layouts: 81.4 us -> 2.06 us
  Pallas kernels: 0 us -> 71.4 us
  matrix products: 41.6 us -> 0 us
  starting transfers between devices: 38 us -> 0 us
  other arithmetic: 29.8 us -> 0 us
  between operations: 13.9 us -> 0.01 us
    ppermute x13 -> x0, waiting for transfers between devices: 115 us -> none  [the longest x11 115 us: partner(): lax.ppermute(array, axis, [(i, i ^ 1 << apart) for i in range(lax.axis_si...]
    pallas_call x0 -> x1, Pallas kernels: none -> 71.4 us  [local(): pl.pallas_call(whole_kernel, out_shape=jax.ShapeDtypeStruct((16, 32, 768)...]
    all_gather x2 -> x0, waiting for transfers between devices: 57.6 us -> none  [the longest x1 57.6 us: local(): lax.all_gather(qkv_weight, 'row', axis=0, tiled=True)]
    slice x16 -> x0, local copies, waits for them, and re-layouts: 44.2 us -> none  [the longest x9 38.1 us: local(): padded[row_tap:row_tap + in_rows - 1:2, col_tap:col_tap + in_cols - 1:2, :]]
    dot_general x26 -> x0, matrix products: 41.6 us -> none  [the longest x12 17.8 us: one_head(): jnp.einsum('qd,kd->qk', query_head, key_head, preferred_element_type=jnp....]
    ppermute x13 -> x0, starting transfers between devices: 38 us -> none  [the longest x11 29.2 us: partner(): lax.ppermute(array, axis, [(i, i ^ 1 << apart) for i in range(lax.axis_si...]
    unnamed x30 -> x1, local copies, waits for them, and re-layouts: 14.7 us -> 2.06 us
    select_n x14 -> x0, other arithmetic: 10.7 us -> none  [the longest x6 5.39 us: split_pair(): send = jnp.where(mine == 0, view[:, 1], view[:, 0])]
  transfers between devices with their start and end apart: 15 -> 0, of which waited for: 11 -> 0; matrix products, arithmetic and copies ran while one was open for 17% -> 0% of each run, Pallas kernels for 0% -> 0%
where the time goes in v2:
time: 74.5 us; the launch traced here: 73.5 us
  Pallas kernels  71.4 us (96%)
  local copies, waits for them, and re-layouts  2.06 us (3%)
    pallas_call x1, Pallas kernels, local(): pl.pallas_call(whole_kernel, out_shape=jax.ShapeDtypeStruct((16, 32, 768)...  71.4 us
    unnamed x1, local copies, waits for them, and re-layouts  2.06 us

profile of v2, /device:TPU:1, one launch (start us, length us, event | category | flops | bytes accessed | tf_op | source)
XLA Modules:
  0.0 73.5 jit_solution(6901401609698649730)
XLA Ops:
  0.0 71.4 %whole.1 = bf16[16,32,768]{2,1,0:T(8,128)(2,1)} custom-call(bf16[32,64,256]{2,1,0:T(8,128)(2,1)} %feat.1, bf16[576,256]{1,0:T(8,128)(2,1)} %cw.1, f32[1,256]{1,0:T(1,128)} %bitcast.1, bf16[6,2304]{1,0:T(8,128)(2,1)} %w6.1, bf16[256,768]{1,0:T(8,128)(2,1)} %proj.1, s32[16,32]{1,0:T(8,128)} %phase.1, s32[16,32]{1,0:T(8,128)} %tissue.1), custom_call_target="tpu_custom_call" | custom-call | tf_op jit(solution)/shard_map/whole/pallas_call | solution.py:437
  71.4 2.1 %copy.9 = bf16[16,32,768]{2,1,0:T(8,128)(2,1)} copy(bf16[16,32,768]{2,1,0:T(8,128)(2,1)} %whole.1) | data formatting | bytes 1572864

commit v3 on v2

--- a/solution.py
+++ b/solution.py
@@ -13,6 +13,8 @@
 PLANE = 16
 NY = 8
 HALF = 1152
+PART = 640
+REST = HALF - PART
 VMEM_LIMIT = 56 * 1024 * 1024
 
 
@@ -56,10 +58,10 @@
 
 def whole_kernel(
     feat, cw, bias, w6, proj, phase, tissue, out,
-    grid_in, ext, halo, top, cwg, wsend, wz, rings, slots, flags, orders,
+    grid_in, ext, halo, top, cwg, wsend, wz, rings, wsend_b, wz_b, rings_b, proj_b, slots, flags, orders,
     fold, gram, keys, values, dead, queries, mixed, theirs,
     cw_send, cw_recv, h_send, h_recv, z_send, z_recv, g_send, g_recv,
-    f_send, f_recv, s_send, s_recv, u_send, u_recv, d_send, d_recv, m_send, m_recv, own_sem,
+    f_send, f_recv, s_send, s_recv, zb_send, zb_recv, u_send, u_recv, m_send, m_recv, own_sem,
 ):
     row, col = lax.axis_index("row"), lax.axis_index("col")
     core = lax.rem(row, 2)
@@ -74,10 +76,18 @@
     above = (lax.rem(row + PLANE, ROWS), col)
     below = (lax.rem(row + ROWS - PLANE, ROWS), col)
     plane = [(base + lax.rem(mine + k, PLANE), col) for k in range(1, PLANE)]
+    z_at = mine // 2
+    pole_at = 2 * y_at + core
+    pole = []
+    for k in range(1, PLANE):
+        other = lax.rem(pole_at + k, PLANE)
+        pole.append((PLANE * (other // 2) + 2 * z_at + lax.rem(other, 2), col))
+    ahead = (base + lax.rem(mine + 2, PLANE), col)
+    behind = (base + lax.rem(mine + PLANE - 2, PLANE), col)
     greet(
         [(row, right), (row, left), (down, col), (up, col), (down, right), (up, left)]
-        + [above, below]
         + plane
+        + pole
     )
 
     part = pl.multiple_of(core * 288, 32)
@@ -100,11 +110,15 @@
     top_copy.start()
 
     for c in range(2):
-        wsend[c] = jnp.zeros((8, HALF), BF16)
-        for j in range(3):
-            wsend[c, 0:6, 384 * j : 384 * j + 384] = w6[
-                :, 768 * j + 384 * c : 768 * j + 384 * c + 384
-            ]
+        wsend[c] = jnp.zeros((8, PART), BF16)
+        wsend_b[c] = jnp.zeros((8, REST), BF16)
+        for n in range(9):
+            at = 768 * (n // 3) + 384 * c + 128 * (n % 3)
+            block = w6[:, at : at + 128]
+            if n < 5:
+                wsend[c, 0:6, 128 * n : 128 * n + 128] = block
+            else:
+                wsend_b[c, 0:6, 128 * n - PART : 128 * n + 128 - PART] = block
     z_copies = []
     for k in range(1, PLANE):
         to_core = lax.rem(core + k, 2)
@@ -113,8 +127,15 @@
         )
         copy.start()
         z_copies.append(copy)
+        copy = remote(
+            wsend_b.at[to_core], wz_b.at[pole_at], zb_send.at[k], zb_recv.at[k], pole[k - 1]
+        )
+        copy.start()
+        z_copies.append(copy)
     own_z = pltpu.make_async_copy(wsend.at[core], wz.at[mine], own_sem.at[1])
     own_z.start()
+    own_y = pltpu.make_async_copy(wsend_b.at[core], wz_b.at[pole_at], own_sem.at[2])
+    own_y.start()
 
     o, c = iota((256, 256), 0), iota((256, 256), 1)
     k, si, sp = o & 7, (o >> 3) & 3, (o >> 5) & 1
@@ -178,24 +199,32 @@
     sib_right.start()
 
     own_z.wait()
+    own_y.wait()
     for copy in z_copies:
         copy.wait_recv()
     o, c = iota((96, 128), 0), iota((96, 128), 1)
     pack = onehot((o == 6 * (c >> 3) + (c & 7)) & ((c & 7) < 6)).astype(BF16)
-    rings[y_at] = dot(pack, wz[...].reshape(128, HALF)).astype(BF16)
-
-    def w_up(t):
-        piece = rings.at[lax.rem(y_at + NY - t, NY)]
-        piece = piece.at[0:48] if t == 3 else piece
-        return remote(piece, piece, u_send.at[t], u_recv.at[t], above)
-
-    def w_down(t):
-        piece = rings.at[lax.rem(y_at + t, NY)]
-        piece = piece.at[48:96] if t == 3 else piece
-        return remote(piece, piece, d_send.at[t], d_recv.at[t], below)
-
-    w_up(0).start()
-    w_down(0).start()
+    rings[y_at] = dot(pack, wz[...].reshape(128, PART)).astype(BF16)
+    rings_b[z_at] = dot(pack, wz_b[...].reshape(128, REST)).astype(BF16)
+
+    def ring(n, t):
+        buffer, at, to = ((rings, y_at, (above, below)), (rings_b, z_at, (ahead, behind)))[n // 2]
+        if n % 2 == 0:
+            piece = buffer.at[lax.rem(at + NY - t, NY)]
+            piece = piece.at[0:48] if t == 3 else piece
+        else:
+            piece = buffer.at[lax.rem(at + t, NY)]
+            piece = piece.at[48:96] if t == 3 else piece
+        return remote(piece, piece, u_send.at[n, t], u_recv.at[n, t], to[n % 2])
+
+    def ring_step(t):
+        for n in range(4):
+            if t > 0:
+                ring(n, t - 1).wait_recv()
+            if t < 4:
+                ring(n, t).start()
+
+    ring_step(0)
 
     top_copy.wait_recv()
     left_copy.wait_recv()
@@ -220,6 +249,18 @@
     keep = jnp.where((iota((17, 8, 256), 0) == 0) & jnp.logical_not(inside), 0.0, keep)
     grid_in[1, 0:17, 1, 0] = jnp.where(first, keep, moved)
 
+    p32 = proj[...].astype(F32)
+    mean_col = jnp.mean(p32, axis=1, keepdims=True)
+    mean_row = dot_nt(jnp.ones((8, 768), BF16), proj[...])[0:1] * (1.0 / 768.0)
+    gram[...] = (dot_nt(proj[...], proj[...]) * (1.0 / 768.0) - mean_col * mean_row).astype(BF16)
+    s_at, d_at = iota((768, 768), 0), iota((1, 768), 1)
+    big = (d_at * 683) >> 16
+    small = ((d_at - 96 * big) * 5462) >> 16
+    swapped = 96 * small + 12 * big + d_at - 96 * big - 12 * small
+    proj_b[...] = dot(proj[...], onehot(s_at == swapped).astype(BF16)).astype(BF16)
+
+    ring_step(1)
+
     on_right.wait_recv()
     sib_on = cw_copy(6, across, 0, 144, sibling)
     sib_on.start()
@@ -302,10 +343,7 @@
             arrived(slot, p).wait_recv()
             f_sib(slot, p).start()
 
-    p32 = proj[...].astype(F32)
-    mean_col = jnp.mean(p32, axis=1, keepdims=True)
-    mean_row = dot_nt(jnp.ones((8, 768), BF16), proj[...])[0:1] * (1.0 / 768.0)
-    gram[...] = (dot_nt(proj[...], proj[...]) * (1.0 / 768.0) - mean_col * mean_row).astype(BF16)
+    ring_step(2)
     for copy in g_copies:
         copy.wait_recv()
     lane128 = iota((512, 128), 1)
@@ -318,27 +356,20 @@
             for h in range(2):
                 dead[:, q, c, 64 * h : 64 * h + 64, :] = gone[h]
 
-    w_up(0).wait_recv()
-    w_up(1).start()
-    w_down(0).wait_recv()
-    w_down(1).start()
+    ring_step(3)
+    ring_step(4)
+    ones8 = jnp.ones((8, 768), BF16)
+    for cut, rows, p_rows in (
+        (slice(0, PART), rings, proj),
+        (slice(PART, HALF), rings_b, proj_b),
+    ):
+        w = rows[...].reshape(768, cut.stop - cut.start)
+        part_fold = dot(p_rows[...], w) - mean_col * dot(ones8, w)[0:1]
+        if cut.start == 0:
+            q_scale = 0.125 * 1.4426950408889634
+            part_fold = part_fold * jnp.where(iota((1, PART), 1) < 384, q_scale, 1.0)
+        fold[:, cut] = part_fold.astype(BF16)
     serve(0)
-    w_up(1).wait_recv()
-    w_up(2).start()
-    w_down(1).wait_recv()
-    w_down(2).start()
-    serve(1)
-    w_up(2).wait_recv()
-    w_up(3).start()
-    w_down(2).wait_recv()
-    w_down(3).start()
-    w_up(3).wait_recv()
-    w_down(3).wait_recv()
-
-    w = rings[...].reshape(768, HALF)
-    col_sum = dot(jnp.ones((8, 768), BF16), w)[0:1]
-    scale = jnp.where(iota((1, HALF), 1) < 384, 0.125 * 1.4426950408889634, 1.0)
-    fold[...] = ((dot(proj[...], w) - mean_col * col_sum) * scale).astype(BF16)
 
     lane = iota((256, 128), 1)
     unit = onehot(lane == 0).astype(BF16)
@@ -362,9 +393,9 @@
         for n in range(3):
             if n == 1:
 
-                @pl.when(p < 2)
+                @pl.when(p < 3)
                 def _():
-                    serve(p + 2)
+                    serve(p + 1)
 
             cut = slice(128 * n, 128 * n + 128)
             k_pair = jnp.concatenate([keys[:, cut], mask], axis=1)
@@ -410,8 +441,8 @@
     ]:
         copy.wait_send()
     for t in range(4):
-        w_up(t).wait_send()
-        w_down(t).wait_send()
+        for n in range(4):
+            ring(n, t).wait_send()
     for p in range(4):
         give(p).wait_send()
         f_two(p).wait_send()
@@ -445,9 +476,13 @@
             pltpu.VMEM((40, 256), BF16),
             pltpu.VMEM((64, 256), BF16),
             pltpu.VMEM((4, 576, 256), BF16),
-            pltpu.VMEM((2, 8, HALF), BF16),
-            pltpu.VMEM((16, 8, HALF), BF16),
-            pltpu.VMEM((NY, 96, HALF), BF16),
+            pltpu.VMEM((2, 8, PART), BF16),
+            pltpu.VMEM((16, 8, PART), BF16),
+            pltpu.VMEM((NY, 96, PART), BF16),
+            pltpu.VMEM((2, 8, REST), BF16),
+            pltpu.VMEM((16, 8, REST), BF16),
+            pltpu.VMEM((NY, 96, REST), BF16),
+            pltpu.VMEM((256, 768), BF16),
             pltpu.VMEM((4, 2, 4, 128, 256), BF16),
             pltpu.VMEM((4, 2, 8, 512), BF16),
             pltpu.VMEM((2, 256, 256), BF16),
@@ -465,10 +500,10 @@
             dma((8,)), dma((8,)),
             dma((4, 4)), dma((4, 4)),
             dma((4, 4)), dma((4, 4)),
+            dma((16,)), dma((16,)),
+            dma((4, 4)), dma((4, 4)),
             dma((4,)), dma((4,)),
-            dma((4,)), dma((4,)),
-            dma((4,)), dma((4,)),
-            dma((2,)),
+            dma((3,)),
         ],
         compiler_params=pltpu.CompilerParams(
             collective_id=0, has_side_effects=True, vmem_limit_bytes=VMEM_LIMIT

time: 74.5 us -> 82.4 us (1.11)
  Pallas kernels: 71.4 us -> 80.1 us
    pallas_call x1, Pallas kernels: 71.4 us -> 80.1 us  [local(): pl.pallas_call(whole_kernel, out_shape=jax.ShapeDtypeStruct((16, 32, 768)...]
where the time goes in v3:
time: 82.4 us; the launch traced here: 82.2 us
  Pallas kernels  80.1 us (97%)
  local copies, waits for them, and re-layouts  2.06 us (2%)
    pallas_call x1, Pallas kernels, local(): pl.pallas_call(whole_kernel, out_shape=jax.ShapeDtypeStruct((16, 32, 768)...  80.1 us
    unnamed x1, local copies, waits for them, and re-layouts  2.06 us

profile of v3, /device:TPU:1, one launch (start us, length us, event | category | flops | bytes accessed | tf_op | source)
XLA Modules:
  0.0 82.2 jit_solution(11990402144400596300)
XLA Ops:
  0.0 80.1 %whole.1 = bf16[16,32,768]{2,1,0:T(8,128)(2,1)} custom-call(bf16[32,64,256]{2,1,0:T(8,128)(2,1)} %feat.1, bf16[576,256]{1,0:T(8,128)(2,1)} %cw.1, f32[1,256]{1,0:T(1,128)} %bitcast.1, bf16[6,2304]{1,0:T(8,128)(2,1)} %w6.1, bf16[256,768]{1,0:T(8,128)(2,1)} %proj.1, s32[16,32]{1,0:T(8,128)} %phase.1, s32[16,32]{1,0:T(8,128)} %tissue.1), custom_call_target="tpu_custom_call" | custom-call | tf_op jit(solution)/shard_map/whole/pallas_call | solution.py:468
  80.1 2.1 %copy.9 = bf16[16,32,768]{2,1,0:T(8,128)(2,1)} copy(bf16[16,32,768]{2,1,0:T(8,128)(2,1)} %whole.1) | data formatting | bytes 1572864

commit v4 on v2

--- a/solution.py
+++ b/solution.py
@@ -12,7 +12,7 @@
 COLS = 4
 PLANE = 16
 NY = 8
-HALF = 1152
+PAIR = 384
 VMEM_LIMIT = 56 * 1024 * 1024
 
 
@@ -57,9 +57,9 @@
 def whole_kernel(
     feat, cw, bias, w6, proj, phase, tissue, out,
     grid_in, ext, halo, top, cwg, wsend, wz, rings, slots, flags, orders,
-    fold, gram, keys, values, dead, queries, mixed, theirs,
+    fold, gram, dead, mixed, theirs,
     cw_send, cw_recv, h_send, h_recv, z_send, z_recv, g_send, g_recv,
-    f_send, f_recv, s_send, s_recv, u_send, u_recv, d_send, d_recv, m_send, m_recv, own_sem,
+    f_send, f_recv, s_send, s_recv, y_send, y_recv, x_send, x_recv, m_send, m_recv, own_sem,
 ):
     row, col = lax.axis_index("row"), lax.axis_index("col")
     core = lax.rem(row, 2)
@@ -71,12 +71,15 @@
     right, left = lax.rem(col + 1, COLS), lax.rem(col + COLS - 1, COLS)
     across = lax.rem(col + 2, COLS)
     down, up = lax.rem(row + 1, ROWS), lax.rem(row + ROWS - 1, ROWS)
-    above = (lax.rem(row + PLANE, ROWS), col)
-    below = (lax.rem(row + ROWS - PLANE, ROWS), col)
+
+    def along_y(step):
+        return (lax.rem(row + PLANE * step + ROWS, ROWS), col)
+
     plane = [(base + lax.rem(mine + k, PLANE), col) for k in range(1, PLANE)]
     greet(
         [(row, right), (row, left), (down, col), (up, col), (down, right), (up, left)]
-        + [above, below]
+        + [(row, across)]
+        + [along_y(step) for step in (1, -1, 2, -2)]
         + plane
     )
 
@@ -99,12 +102,12 @@
     top_copy = remote(feat.at[31], top, h_send.at[0], h_recv.at[0], (down, col))
     top_copy.start()
 
+    group = lax.rem(col, 3)
     for c in range(2):
-        wsend[c] = jnp.zeros((8, HALF), BF16)
+        wsend[c] = jnp.zeros((8, PAIR), BF16)
         for j in range(3):
-            wsend[c, 0:6, 384 * j : 384 * j + 384] = w6[
-                :, 768 * j + 384 * c : 768 * j + 384 * c + 384
-            ]
+            at = pl.multiple_of(768 * j + 384 * c + 128 * group, 128)
+            wsend[c, 0:6, 128 * j : 128 * j + 128] = w6[:, pl.ds(at, 128)]
     z_copies = []
     for k in range(1, PLANE):
         to_core = lax.rem(core + k, 2)
@@ -166,6 +169,11 @@
                 copy.start()
                 g_copies.append(copy)
 
+    p32 = proj[...].astype(F32)
+    mean_col = jnp.mean(p32, axis=1, keepdims=True)
+    mean_row = dot_nt(jnp.ones((8, 768), BF16), proj[...])[0:1] * (1.0 / 768.0)
+    gram[...] = (dot_nt(proj[...], proj[...]) * (1.0 / 768.0) - mean_col * mean_row).astype(BF16)
+
     to_right.wait_recv()
     on_right = cw_copy(2, left, 0, 144, (row, right))
     on_right.start()
@@ -182,20 +190,15 @@
         copy.wait_recv()
     o, c = iota((96, 128), 0), iota((96, 128), 1)
     pack = onehot((o == 6 * (c >> 3) + (c & 7)) & ((c & 7) < 6)).astype(BF16)
-    rings[y_at] = dot(pack, wz[...].reshape(128, HALF)).astype(BF16)
-
-    def w_up(t):
-        piece = rings.at[lax.rem(y_at + NY - t, NY)]
-        piece = piece.at[0:48] if t == 3 else piece
-        return remote(piece, piece, u_send.at[t], u_recv.at[t], above)
-
-    def w_down(t):
-        piece = rings.at[lax.rem(y_at + t, NY)]
-        piece = piece.at[48:96] if t == 3 else piece
-        return remote(piece, piece, d_send.at[t], d_recv.at[t], below)
-
-    w_up(0).start()
-    w_down(0).start()
+    rings[y_at] = dot(pack, wz[...].reshape(128, PAIR)).astype(BF16)
+
+    def y_copy(i, start, size, behind, step):
+        piece = rings.at[lax.rem(y_at - behind + NY, NY), start : start + size]
+        return remote(piece, piece, y_send.at[i], y_recv.at[i], along_y(step))
+
+    y_near = [y_copy(i, 0, 96, 0, step) for i, step in enumerate((2, -2, 1, -1))]
+    for copy in y_near:
+        copy.start()
 
     top_copy.wait_recv()
     left_copy.wait_recv()
@@ -241,7 +244,10 @@
                 pieces.append(window.reshape(256, 256).astype(BF16))
         pre = dot(jnp.concatenate(pieces, axis=1), weights) + bias[...]
         features = jax.nn.gelu(pre).astype(BF16)
-        placed = dot(orders[h], features).astype(BF16).reshape(4, 64, 256)
+        f32 = features.astype(F32)
+        spread_rows = jnp.sum(dot(features, gram[...]) * f32, axis=1, keepdims=True)
+        f32 = f32 * lax.rsqrt(jnp.maximum(spread_rows, 0.0) + 1e-05)
+        placed = dot(orders[h], f32.astype(BF16)).astype(BF16).reshape(4, 64, 256)
         slots[0, 0, :, 64 * h : 64 * h + 64, :] = placed
 
     def f_right(p):
@@ -302,10 +308,16 @@
             arrived(slot, p).wait_recv()
             f_sib(slot, p).start()
 
-    p32 = proj[...].astype(F32)
-    mean_col = jnp.mean(p32, axis=1, keepdims=True)
-    mean_row = dot_nt(jnp.ones((8, 768), BF16), proj[...])[0:1] * (1.0 / 768.0)
-    gram[...] = (dot_nt(proj[...], proj[...]) * (1.0 / 768.0) - mean_col * mean_row).astype(BF16)
+    y_near[0].wait_recv()
+    y_far = [y_copy(4, 0, 96, 2, 1), y_copy(6, 0, 48, 2, 2)]
+    for copy in y_far:
+        copy.start()
+    y_near[1].wait_recv()
+    y_back = [y_copy(5, 0, 96, -2, -1), y_copy(7, 48, 48, -2, -2)]
+    for copy in y_back:
+        copy.start()
+    y_far = y_far + y_back
+
     for copy in g_copies:
         copy.wait_recv()
     lane128 = iota((512, 128), 1)
@@ -318,27 +330,24 @@
             for h in range(2):
                 dead[:, q, c, 64 * h : 64 * h + 64, :] = gone[h]
 
-    w_up(0).wait_recv()
-    w_up(1).start()
-    w_down(0).wait_recv()
-    w_down(1).start()
+    for copy in y_near[2:] + y_far:
+        copy.wait_recv()
+    w = rings[...].reshape(768, PAIR)
+    folded = dot(proj[...], w) - mean_col * dot(jnp.ones((8, 768), BF16), w)[0:1]
+    scale = jnp.where(iota((1, PAIR), 1) < 128, 0.125 * 1.4426950408889634, 1.0)
+    fold[group] = (folded * scale).astype(BF16)
+
+    x_copies = [
+        (a, remote(fold.at[a % 3], fold.at[a % 3], x_send.at[b], x_recv.at[a % 3], (row, b)))
+        for a, b in ((0, 1), (1, 0), (1, 2), (1, 3), (2, 1), (2, 3), (2, 0), (3, 2))
+    ]
+    for a, copy in x_copies:
+        pl.when(col == a)(copy.start)
     serve(0)
-    w_up(1).wait_recv()
-    w_up(2).start()
-    w_down(1).wait_recv()
-    w_down(2).start()
-    serve(1)
-    w_up(2).wait_recv()
-    w_up(3).start()
-    w_down(2).wait_recv()
-    w_down(3).start()
-    w_up(3).wait_recv()
-    w_down(3).wait_recv()
-
-    w = rings[...].reshape(768, HALF)
-    col_sum = dot(jnp.ones((8, 768), BF16), w)[0:1]
-    scale = jnp.where(iota((1, HALF), 1) < 384, 0.125 * 1.4426950408889634, 1.0)
-    fold[...] = ((dot(proj[...], w) - mean_col * col_sum) * scale).astype(BF16)
+    for g in range(3):
+        pl.when(group != g)(remote(
+            fold.at[g], fold.at[g], x_send.at[0], x_recv.at[g], sibling
+        ).wait_recv)
 
     lane = iota((256, 128), 1)
     unit = onehot(lane == 0).astype(BF16)
@@ -351,25 +360,19 @@
         for slot in range(4):
             f_sib(slot, p).wait_recv()
         x = slots[:, :, p].reshape(1024, 256)
-        y = dot(x, gram[...])
-        var = jnp.sum(y * x.astype(F32), axis=1, keepdims=True)
-        rstd = lax.rsqrt(jnp.maximum(var, 0.0) + 1e-05)
-        kv = (dot(x, fold[:, 384:]) * rstd).astype(BF16)
-        keys[...] = kv[:, 0:384]
-        values[...] = kv[:, 384:768]
-        queries[...] = (dot(x[0:256], fold[:, 0:384]) * rstd[0:256]).astype(BF16)
         mask = dead[p].reshape(1024, 128)
         for n in range(3):
             if n == 1:
 
-                @pl.when(p < 2)
+                @pl.when(p < 3)
                 def _():
-                    serve(p + 2)
+                    serve(p + 1)
 
             cut = slice(128 * n, 128 * n + 128)
-            k_pair = jnp.concatenate([keys[:, cut], mask], axis=1)
-            v_pair = jnp.concatenate([values[:, cut], ones], axis=1)
-            q_pair = queries[:, cut].astype(F32)
+            kv = dot(x, fold[n, :, 128:384]).astype(BF16)
+            k_pair = jnp.concatenate([kv[:, 0:128], mask], axis=1)
+            v_pair = jnp.concatenate([kv[:, 128:256], ones], axis=1)
+            q_pair = dot(x[0:256], fold[n, :, 0:128])
             both = []
             for e in range(2):
                 q_head = jnp.where((lane >= 64) == (e == 1), q_pair, 0.0).astype(BF16)
@@ -409,9 +412,10 @@
         top_copy, left_copy, corner_copy,
     ]:
         copy.wait_send()
-    for t in range(4):
-        w_up(t).wait_send()
-        w_down(t).wait_send()
+    for copy in y_near + y_far:
+        copy.wait_send()
+    for a, copy in x_copies:
+        pl.when(col == a)(copy.wait_send)
     for p in range(4):
         give(p).wait_send()
         f_two(p).wait_send()
@@ -445,18 +449,15 @@
             pltpu.VMEM((40, 256), BF16),
             pltpu.VMEM((64, 256), BF16),
             pltpu.VMEM((4, 576, 256), BF16),
-            pltpu.VMEM((2, 8, HALF), BF16),
-            pltpu.VMEM((16, 8, HALF), BF16),
-            pltpu.VMEM((NY, 96, HALF), BF16),
+            pltpu.VMEM((2, 8, PAIR), BF16),
+            pltpu.VMEM((16, 8, PAIR), BF16),
+            pltpu.VMEM((NY, 96, PAIR), BF16),
             pltpu.VMEM((4, 2, 4, 128, 256), BF16),
             pltpu.VMEM((4, 2, 8, 512), BF16),
             pltpu.VMEM((2, 256, 256), BF16),
-            pltpu.VMEM((256, HALF), BF16),
+            pltpu.VMEM((3, 256, PAIR), BF16),
             pltpu.VMEM((256, 256), BF16),
-            pltpu.VMEM((1024, 384), BF16),
-            pltpu.VMEM((1024, 384), BF16),
             pltpu.VMEM((4, 4, 2, 128, 128), BF16),
-            pltpu.VMEM((256, 384), BF16),
             pltpu.VMEM((4, 256, 384), BF16),
             pltpu.VMEM((4, 128, 384), BF16),
             dma((8,)), dma((8,)),
@@ -465,8 +466,8 @@
             dma((8,)), dma((8,)),
             dma((4, 4)), dma((4, 4)),
             dma((4, 4)), dma((4, 4)),
-            dma((4,)), dma((4,)),
-            dma((4,)), dma((4,)),
+            dma((8,)), dma((8,)),
+            dma((4,)), dma((3,)),
             dma((4,)), dma((4,)),
             dma((2,)),
         ],

time: 74.5 us -> 70.5 us (0.946); the launches traced: 73.5 us -> 70.3 us
  Pallas kernels: 71.4 us -> 68.2 us
    pallas_call x1, Pallas kernels: 71.4 us -> 68.2 us  [local(): pl.pallas_call(whole_kernel, out_shape=jax.ShapeDtypeStruct((16, 32, 768)...]
where the time goes in v4:
time: 70.5 us; the launch traced here: 70.3 us
  Pallas kernels  68.2 us (97%)
  local copies, waits for them, and re-layouts  2.06 us (3%)
    pallas_call x1, Pallas kernels, local(): pl.pallas_call(whole_kernel, out_shape=jax.ShapeDtypeStruct((16, 32, 768)...  68.2 us
    unnamed x1, local copies, waits for them, and re-layouts  2.06 us

profile of v4, /device:TPU:1, one launch (start us, length us, event | category | flops | bytes accessed | tf_op | source)
XLA Modules:
  0.0 70.3 jit_solution(14432614836047026464)
XLA Ops:
  0.0 68.2 %whole.1 = bf16[16,32,768]{2,1,0:T(8,128)(2,1)} custom-call(bf16[32,64,256]{2,1,0:T(8,128)(2,1)} %feat.1, bf16[576,256]{1,0:T(8,128)(2,1)} %cw.1, f32[1,256]{1,0:T(1,128)} %bitcast.1, bf16[6,2304]{1,0:T(8,128)(2,1)} %w6.1, bf16[256,768]{1,0:T(8,128)(2,1)} %proj.1, s32[16,32]{1,0:T(8,128)} %phase.1, s32[16,32]{1,0:T(8,128)} %tissue.1), custom_call_target="tpu_custom_call" | custom-call | tf_op jit(solution)/shard_map/whole/pallas_call | solution.py:441
  68.2 2.1 %copy.9 = bf16[16,32,768]{2,1,0:T(8,128)(2,1)} copy(bf16[16,32,768]{2,1,0:T(8,128)(2,1)} %whole.1) | data formatting | bytes 1572864

commit v5 on v4

--- a/solution.py
+++ b/solution.py
@@ -141,6 +141,32 @@
         ext.at[24:32], halo.at[32:40], h_send.at[2], h_recv.at[2], (down, right)
     )
     corner_copy.start()
+
+    own_z.wait()
+    for copy in z_copies:
+        copy.wait_recv()
+    o, c = iota((96, 128), 0), iota((96, 128), 1)
+    pack = onehot((o == 6 * (c >> 3) + (c & 7)) & ((c & 7) < 6)).astype(BF16)
+    rings[y_at] = dot(pack, wz[...].reshape(128, PAIR)).astype(BF16)
+
+    def y_copy(i, start, size, behind, step):
+        piece = rings.at[lax.rem(y_at - behind + NY, NY), start : start + size]
+        return remote(piece, piece, y_send.at[i], y_recv.at[i], along_y(step))
+
+    y_near = [y_copy(i, 0, 96, 0, step) for i, step in enumerate((2, -2, 1, -1))]
+    for copy in y_near:
+        copy.start()
+
+    to_right.wait_recv()
+    on_right = cw_copy(2, left, 0, 144, (row, right))
+    on_right.start()
+    sib_left = cw_copy(4, left, 0, 288, sibling)
+    sib_left.start()
+    to_left.wait_recv()
+    on_left = cw_copy(3, right, 144, 144, (row, left))
+    on_left.start()
+    sib_right = cw_copy(5, right, 0, 288, sibling)
+    sib_right.start()
 
     lane, sub = iota((8, 256), 1), iota((8, 256), 0)
     for h in range(2):
@@ -174,32 +200,6 @@
     mean_row = dot_nt(jnp.ones((8, 768), BF16), proj[...])[0:1] * (1.0 / 768.0)
     gram[...] = (dot_nt(proj[...], proj[...]) * (1.0 / 768.0) - mean_col * mean_row).astype(BF16)
 
-    to_right.wait_recv()
-    on_right = cw_copy(2, left, 0, 144, (row, right))
-    on_right.start()
-    sib_left = cw_copy(4, left, 0, 288, sibling)
-    sib_left.start()
-    to_left.wait_recv()
-    on_left = cw_copy(3, right, 144, 144, (row, left))
-    on_left.start()
-    sib_right = cw_copy(5, right, 0, 288, sibling)
-    sib_right.start()
-
-    own_z.wait()
-    for copy in z_copies:
-        copy.wait_recv()
-    o, c = iota((96, 128), 0), iota((96, 128), 1)
-    pack = onehot((o == 6 * (c >> 3) + (c & 7)) & ((c & 7) < 6)).astype(BF16)
-    rings[y_at] = dot(pack, wz[...].reshape(128, PAIR)).astype(BF16)
-
-    def y_copy(i, start, size, behind, step):
-        piece = rings.at[lax.rem(y_at - behind + NY, NY), start : start + size]
-        return remote(piece, piece, y_send.at[i], y_recv.at[i], along_y(step))
-
-    y_near = [y_copy(i, 0, 96, 0, step) for i, step in enumerate((2, -2, 1, -1))]
-    for copy in y_near:
-        copy.start()
-
     top_copy.wait_recv()
     left_copy.wait_recv()
     corner_copy.wait_recv()
@@ -233,6 +233,16 @@
     for copy in (sib_left, sib_right, sib_on, sib_off):
         copy.wait_recv()
 
+    y_near[0].wait_recv()
+    y_far = [y_copy(4, 0, 96, 2, 1), y_copy(6, 0, 48, 2, 2)]
+    for copy in y_far:
+        copy.start()
+    y_near[1].wait_recv()
+    y_back = [y_copy(5, 0, 96, -2, -1), y_copy(7, 48, 48, -2, -2)]
+    for copy in y_back:
+        copy.start()
+    y_far = y_far + y_back
+
     weights = cwg[...].reshape(2304, 256)
     for h in range(2):
         pieces = []
@@ -308,16 +318,19 @@
             arrived(slot, p).wait_recv()
             f_sib(slot, p).start()
 
-    y_near[0].wait_recv()
-    y_far = [y_copy(4, 0, 96, 2, 1), y_copy(6, 0, 48, 2, 2)]
-    for copy in y_far:
-        copy.start()
-    y_near[1].wait_recv()
-    y_back = [y_copy(5, 0, 96, -2, -1), y_copy(7, 48, 48, -2, -2)]
-    for copy in y_back:
-        copy.start()
-    y_far = y_far + y_back
-
+    for copy in y_near[2:] + y_far:
+        copy.wait_recv()
+    w = rings[...].reshape(768, PAIR)
+    folded = dot(proj[...], w) - mean_col * dot(jnp.ones((8, 768), BF16), w)[0:1]
+    scale = jnp.where(iota((1, PAIR), 1) < 128, 0.125 * 1.4426950408889634, 1.0)
+    fold[group] = (folded * scale).astype(BF16)
+
+    x_copies = [
+        (a, remote(fold.at[a % 3], fold.at[a % 3], x_send.at[b], x_recv.at[a % 3], (row, b)))
+        for a, b in ((0, 1), (1, 0), (1, 2), (1, 3), (2, 1), (2, 3), (2, 0), (3, 2))
+    ]
+    for a, copy in x_copies:
+        pl.when(col == a)(copy.start)
     for copy in g_copies:
         copy.wait_recv()
     lane128 = iota((512, 128), 1)
@@ -330,62 +343,73 @@
             for h in range(2):
                 dead[:, q, c, 64 * h : 64 * h + 64, :] = gone[h]
 
-    for copy in y_near[2:] + y_far:
-        copy.wait_recv()
-    w = rings[...].reshape(768, PAIR)
-    folded = dot(proj[...], w) - mean_col * dot(jnp.ones((8, 768), BF16), w)[0:1]
-    scale = jnp.where(iota((1, PAIR), 1) < 128, 0.125 * 1.4426950408889634, 1.0)
-    fold[group] = (folded * scale).astype(BF16)
-
-    x_copies = [
-        (a, remote(fold.at[a % 3], fold.at[a % 3], x_send.at[b], x_recv.at[a % 3], (row, b)))
-        for a, b in ((0, 1), (1, 0), (1, 2), (1, 3), (2, 1), (2, 3), (2, 0), (3, 2))
-    ]
-    for a, copy in x_copies:
-        pl.when(col == a)(copy.start)
     serve(0)
+    lane = iota((256, 128), 1)
+    unit = onehot(iota((512, 128), 1) == 0).astype(BF16)
+    ones = jnp.ones((16, 1024), BF16)
+
+    def give(p):
+        return remote(mixed.at[p, :, 128:256], theirs.at[p], m_send.at[p], m_recv.at[p], sibling)
+
+    def item(p, n):
+        x = slots[:, :, p].reshape(1024, 256)
+        mask = dead[p].reshape(1024, 128)
+        kv = dot(x, fold[n, :, 128:384])
+        keys = jnp.concatenate([kv[:, 0:128].astype(BF16), mask], axis=1)
+        values = jnp.concatenate([kv[:, 128:256].T.astype(BF16), ones], axis=0)
+        q_pair = dot(x[0:256], fold[n, :, 0:128])
+        heads = jnp.concatenate(
+            [jnp.where(lane < 64, q_pair, 0.0), jnp.where(lane < 64, 0.0, q_pair)], axis=0
+        ).astype(BF16)
+        scores = dot_nt(keys, jnp.concatenate([heads, unit], axis=1))
+        highest = jnp.max(scores, axis=0, keepdims=True)
+        weights = jnp.exp2(scores - highest).astype(BF16)
+        result = dot(values, weights)
+        result = result[0:128] / result[128:129]
+        upper = iota((128, 256), 0) < 64
+        mixed[p, n] = jnp.where(upper, result[:, 0:256], result[:, 256:512]).T.astype(BF16)
+
+    def first(p):
+        for slot in range(4):
+            f_sib(slot, p).wait_recv()
+        item(p, group)
+
+    def early(p, carry):
+        first(p)
+
+        @pl.when(p == 0)
+        def _():
+            serve(1)
+
+        return carry
+
+    lax.fori_loop(0, 2, early, 0)
+
     for g in range(3):
         pl.when(group != g)(remote(
             fold.at[g], fold.at[g], x_send.at[0], x_recv.at[g], sibling
         ).wait_recv)
 
-    lane = iota((256, 128), 1)
-    unit = onehot(lane == 0).astype(BF16)
-    ones = jnp.ones((1024, 128), BF16)
-
-    def give(p):
-        return remote(mixed.at[p, 128:256], theirs.at[p], m_send.at[p], m_recv.at[p], sibling)
-
-    def one_phase(p, carry):
-        for slot in range(4):
-            f_sib(slot, p).wait_recv()
-        x = slots[:, :, p].reshape(1024, 256)
-        mask = dead[p].reshape(1024, 128)
-        for n in range(3):
-            if n == 1:
-
-                @pl.when(p < 3)
-                def _():
-                    serve(p + 1)
-
-            cut = slice(128 * n, 128 * n + 128)
-            kv = dot(x, fold[n, :, 128:384]).astype(BF16)
-            k_pair = jnp.concatenate([kv[:, 0:128], mask], axis=1)
-            v_pair = jnp.concatenate([kv[:, 128:256], ones], axis=1)
-            q_pair = dot(x[0:256], fold[n, :, 0:128])
-            both = []
-            for e in range(2):
-                q_head = jnp.where((lane >= 64) == (e == 1), q_pair, 0.0).astype(BF16)
-                scores = dot_nt(jnp.concatenate([q_head, unit], axis=1), k_pair)
-                highest = jnp.max(scores, axis=1, keepdims=True)
-                weights = jnp.exp2(scores - highest).astype(BF16)
-                result = dot(weights, v_pair)
-                both.append(result[:, 0:128] / result[:, 128:256])
-            mixed[p, :, cut] = jnp.where(lane < 64, both[0], both[1]).astype(BF16)
+    def late(p, carry):
+        @pl.when(p >= 2)
+        def _():
+            first(p)
+
+        @pl.when(p == 2)
+        def _():
+            serve(3)
+
+        item(p, lax.rem(group + 1, 3))
+
+        @pl.when(p == 0)
+        def _():
+            serve(2)
+
+        item(p, lax.rem(group + 2, 3))
         give(p).start()
         return carry
 
-    lax.fori_loop(0, 4, one_phase, 0)
+    lax.fori_loop(0, 4, late, 0)
 
     back = []
     j, lane = iota((32, 256), 0), iota((32, 256), 1)
@@ -399,9 +423,13 @@
     for p in range(4):
         give(p).wait_recv()
     for h in range(2):
-        a = mixed[:, 64 * h : 64 * h + 64].reshape(256, 384)
-        b = theirs[:, 64 * h : 64 * h + 64].reshape(256, 384)
-        a, b = dot(back[h], a), dot(back[h], b)
+        a, b = (
+            jnp.concatenate(
+                [dot(back[h], m[:, n, 64 * h : 64 * h + 64].reshape(256, 128)) for n in range(3)],
+                axis=1,
+            )
+            for m in (mixed, theirs)
+        )
         lower = jnp.where(core == 0, a, b).astype(BF16).reshape(8, 32, 384)
         upper = jnp.where(core == 0, b, a).astype(BF16).reshape(8, 32, 384)
         out[8 * h : 8 * h + 8, :, 0:384] = lower
@@ -458,8 +486,8 @@
             pltpu.VMEM((3, 256, PAIR), BF16),
             pltpu.VMEM((256, 256), BF16),
             pltpu.VMEM((4, 4, 2, 128, 128), BF16),
-            pltpu.VMEM((4, 256, 384), BF16),
-            pltpu.VMEM((4, 128, 384), BF16),
+            pltpu.VMEM((4, 3, 256, 128), BF16),
+            pltpu.VMEM((4, 3, 128, 128), BF16),
             dma((8,)), dma((8,)),
             dma((3,)), dma((3,)),
             dma((16,)), dma((16,)),

time: 70.5 us -> 68.7 us (0.974)
  Pallas kernels: 68.2 us -> 66.5 us
    pallas_call x1, Pallas kernels: 68.2 us -> 66.5 us  [local(): pl.pallas_call(whole_kernel, out_shape=jax.ShapeDtypeStruct((16, 32, 768)...]
where the time goes in v5:
time: 68.7 us; the launch traced here: 68.6 us
  Pallas kernels  66.5 us (97%)
  local copies, waits for them, and re-layouts  2.06 us (3%)
    pallas_call x1, Pallas kernels, local(): pl.pallas_call(whole_kernel, out_shape=jax.ShapeDtypeStruct((16, 32, 768)...  66.5 us
    unnamed x1, local copies, waits for them, and re-layouts  2.06 us

profile of v5, /device:TPU:1, one launch (start us, length us, event | category | flops | bytes accessed | tf_op | source)
XLA Modules:
  0.0 68.6 jit_solution(4281712479284673837)
XLA Ops:
  0.0 66.5 %whole.1 = bf16[16,32,768]{2,1,0:T(8,128)(2,1)} custom-call(bf16[32,64,256]{2,1,0:T(8,128)(2,1)} %feat.1, bf16[576,256]{1,0:T(8,128)(2,1)} %cw.1, f32[1,256]{1,0:T(1,128)} %bitcast.1, bf16[6,2304]{1,0:T(8,128)(2,1)} %w6.1, bf16[256,768]{1,0:T(8,128)(2,1)} %proj.1, s32[16,32]{1,0:T(8,128)} %phase.1, s32[16,32]{1,0:T(8,128)} %tissue.1), custom_call_target="tpu_custom_call" | custom-call | tf_op jit(solution)/shard_map/whole/pallas_call | solution.py:469
  66.5 2.1 %copy.9 = bf16[16,32,768]{2,1,0:T(8,128)(2,1)} copy(bf16[16,32,768]{2,1,0:T(8,128)(2,1)} %whole.1) | data formatting | bytes 1572864

commit v6 on v5

--- a/solution.py
+++ b/solution.py
@@ -391,25 +391,23 @@
         ).wait_recv)
 
     def late(p, carry):
-        @pl.when(p >= 2)
-        def _():
-            first(p)
-
-        @pl.when(p == 2)
-        def _():
-            serve(3)
-
-        item(p, lax.rem(group + 1, 3))
-
-        @pl.when(p == 0)
-        def _():
-            serve(2)
-
-        item(p, lax.rem(group + 2, 3))
+        serve(p + 2)
+        for k in (1, 2):
+            item(p, lax.rem(group + k, 3))
         give(p).start()
         return carry
 
-    lax.fori_loop(0, 4, late, 0)
+    lax.fori_loop(0, 2, late, 0)
+
+    def last(p, carry):
+        for slot in range(4):
+            f_sib(slot, p).wait_recv()
+        for k in range(3):
+            item(p, lax.rem(group + k, 3))
+        give(p).start()
+        return carry
+
+    lax.fori_loop(2, 4, last, 0)
 
     back = []
     j, lane = iota((32, 256), 0), iota((32, 256), 1)

time: 68.7 us -> 68.5 us (level)
  no operation moved by 1% of the time
where the time goes in v6:
time: 68.5 us; the launch traced here: 68.3 us
  Pallas kernels  66.2 us (97%)
  local copies, waits for them, and re-layouts  2.06 us (3%)
    pallas_call x1, Pallas kernels, local(): pl.pallas_call(whole_kernel, out_shape=jax.ShapeDtypeStruct((16, 32, 768)...  66.2 us
    unnamed x1, local copies, waits for them, and re-layouts  2.06 us

profile of v6, /device:TPU:1, one launch (start us, length us, event | category | flops | bytes accessed | tf_op | source)
XLA Modules:
  0.0 68.3 jit_solution(6224350728347961979)
XLA Ops:
  0.0 66.2 %whole.1 = bf16[16,32,768]{2,1,0:T(8,128)(2,1)} custom-call(bf16[32,64,256]{2,1,0:T(8,128)(2,1)} %feat.1, bf16[576,256]{1,0:T(8,128)(2,1)} %cw.1, f32[1,256]{1,0:T(1,128)} %bitcast.1, bf16[6,2304]{1,0:T(8,128)(2,1)} %w6.1, bf16[256,768]{1,0:T(8,128)(2,1)} %proj.1, s32[16,32]{1,0:T(8,128)} %phase.1, s32[16,32]{1,0:T(8,128)} %tissue.1), custom_call_target="tpu_custom_call" | custom-call | tf_op jit(solution)/shard_map/whole/pallas_call | solution.py:467
  66.2 2.1 %copy.9 = bf16[16,32,768]{2,1,0:T(8,128)(2,1)} copy(bf16[16,32,768]{2,1,0:T(8,128)(2,1)} %whole.1) | data formatting | bytes 1572864

commit v7 on v6

--- a/solution.py
+++ b/solution.py
@@ -294,6 +294,7 @@
         return remote(piece, piece, f_send.at[0, p], f_recv.at[slot, p], sibling)
 
     for p in range(4):
+        f_two(p).start()
 
         @pl.when(place < 3)
         def _():
@@ -303,7 +304,6 @@
         def _():
             f_left(p).start()
 
-        f_two(p).start()
         f_sib(0, p).start()
 
     def serve(p):

time: 68.5 us -> 68 us (level)
  no operation moved by 1% of the time
where the time goes in v7:
time: 68 us; the launch traced here: 67.8 us
  Pallas kernels  65.7 us (97%)
  local copies, waits for them, and re-layouts  2.06 us (3%)
    pallas_call x1, Pallas kernels, local(): pl.pallas_call(whole_kernel, out_shape=jax.ShapeDtypeStruct((16, 32, 768)...  65.7 us
    unnamed x1, local copies, waits for them, and re-layouts  2.06 us

profile of v7, /device:TPU:1, one launch (start us, length us, event | category | flops | bytes accessed | tf_op | source)
XLA Modules:
  0.0 67.8 jit_solution(12983107122341239200)
XLA Ops:
  0.0 65.7 %whole.1 = bf16[16,32,768]{2,1,0:T(8,128)(2,1)} custom-call(bf16[32,64,256]{2,1,0:T(8,128)(2,1)} %feat.1, bf16[576,256]{1,0:T(8,128)(2,1)} %cw.1, f32[1,256]{1,0:T(1,128)} %bitcast.1, bf16[6,2304]{1,0:T(8,128)(2,1)} %w6.1, bf16[256,768]{1,0:T(8,128)(2,1)} %proj.1, s32[16,32]{1,0:T(8,128)} %phase.1, s32[16,32]{1,0:T(8,128)} %tissue.1), custom_call_target="tpu_custom_call" | custom-call | tf_op jit(solution)/shard_map/whole/pallas_call | solution.py:467
  65.7 2.1 %copy.9 = bf16[16,32,768]{2,1,0:T(8,128)(2,1)} copy(bf16[16,32,768]{2,1,0:T(8,128)(2,1)} %whole.1) | data formatting | bytes 1572864
